TPU v7x, 128 devices: a whole 4x4x4 slice. The times are simulated.
128 devices in a mesh: rep: 32 (over x, z, core), layer: 4 (over y).
Axes of the slice: x: 4, y: 4, z: 4, core: 2. Of those that a mesh axis runs over, the one named last changes fastest.
Arguments:
- activations: bfloat16 [4, 16384, 8192], P('layer', 'rep'), may hold values from -6 to 6
- output_grads: bfloat16 [4, 16384, 8192], P('layer', 'rep'), may hold values from -6 to 6
- in_projection: bfloat16 [4, 32, 8192], P('layer'), may hold values from -0.0625 to 0.0625
- out_projection: bfloat16 [4, 32, 8192], P('layer'), may hold values from -0.0625 to 0.0625
- segment_ids: int32 [16384], P('rep'), may hold values from -1 to 61, as said below
- move_list: int32 [1984], P('rep'), may hold values from -1 to 1023, as said below
Outputs:
- factor: float32 [4, 1024, 1024], P('layer')
- features: bfloat16 [4, 1024, 1024], P('layer', 'rep')
- self_influence: float32 [1024], P('rep')
Inputs may be any that keep to these rules, and one draw needn't show every extreme that they name: `segment_ids`: within each replica's 512 tokens the values never fall; a run of equal values is one document; -1 marks tokens continuing the previous replica's last document and never occurs on replica 0; n documents start on a replica with values 0 to n - 1, n from 2 to 62, and some replica has exactly 62; all documents together are 1024; the last document ends at the end of the last replica. `move_list`: replica r's block of 62 entries gives for its documents in order of their first token (the one continuing onto replica r + 1 included) the destination row in 0 to 1023, and -1 past its last document; every row is named exactly once; the documents of replica r go to rows of replica r - 1, r or r + 1 (rows m * 32 to m * 32 + 31 belong to replica m).
All inputs are finite; a program needn't handle non-finite values.
Results may differ from a plain program's by a relative error of at most 0.0064.
Values may be sent and summed in bfloat16 or wider, within the bound.
A program may use at most 128 MiB of HBM per device.

v0:
```python
import jax
import jax.numpy as jnp
from jax import lax
from jax.sharding import PartitionSpec as P

BAL = 32


DAMPING = 0.05


def shifted(block, axis, distance):
    devices = range(lax.axis_size(axis))
    route = [(i - distance, i) for i in devices if i - distance in devices]
    return lax.ppermute(block, axis, route)


def on_device(activations, output_grads, in_projection, out_projection, segment_ids, move_list):
    contract = (((1,), (1,)), ((), ()))
    left = lax.dot_general(
        in_projection[0], activations[0], contract, preferred_element_type=jnp.float32
    ).astype(jnp.bfloat16)
    right = lax.dot_general(
        out_projection[0], output_grads[0], contract, preferred_element_type=jnp.float32
    ).astype(jnp.bfloat16)
    doc_slots = move_list.shape[0]
    width = left.shape[0] * right.shape[0]
    slot_ids = jnp.arange(doc_slots + 1, dtype=jnp.int32) - 1
    member = (segment_ids[None, :] == slot_ids[:, None]).astype(jnp.bfloat16)
    masked = member[:, None, :] * left[None, :, :]
    blocks = lax.dot_general(
        masked, right, (((2,), (1,)), ((), ())), preferred_element_type=jnp.float32
    )
    sums = blocks.reshape(doc_slots + 1, width)
    counts = jnp.sum(member.astype(jnp.float32), axis=1)
    carried_sum, carried_count = shifted((sums[:1], counts[:1]), "rep", -1)
    last_slot = jnp.max(segment_ids)
    takes = (slot_ids[1:] == last_slot).astype(jnp.float32)
    totals = sums[1:] + takes[:, None] * carried_sum
    lengths = counts[1:] + takes * carried_count[0]
    safe_len = jnp.maximum(lengths, 1.0)
    local_features = (totals / jnp.sqrt(safe_len)[:, None]).astype(jnp.bfloat16)
    replica = lax.axis_index("rep")
    n_rep = lax.axis_size("rep")
    offsets = jnp.where(move_list >= 0, move_list // BAL - replica, 5)
    within = move_list % BAL
    row_ids = jnp.arange(BAL, dtype=jnp.int32)

    def arrange(step_offset):
        select = ((offsets[None, :] == step_offset) & (within[None, :] == row_ids[:, None])).astype(
            jnp.bfloat16
        )
        return jnp.dot(select, local_features, preferred_element_type=jnp.float32).astype(
            jnp.bfloat16
        )

    staying = arrange(0)
    from_right = shifted(arrange(-1), "rep", -1)
    from_left = shifted(arrange(1), "rep", 1)
    mine = (
        staying.astype(jnp.float32) + from_right.astype(jnp.float32) + from_left.astype(jnp.float32)
    ).astype(jnp.bfloat16)
    rows_contract = (((0,), (0,)), ((), ()))
    local_gram = lax.dot_general(mine, mine, rows_contract, preferred_element_type=jnp.float32)
    gram = lax.psum(local_gram, "rep")
    total_docs = BAL * n_rep
    hessian = gram / total_docs + DAMPING * jnp.eye(width, dtype=jnp.float32)
    lower = jnp.linalg.cholesky(hessian)
    solved = lax.linalg.triangular_solve(
        lower, mine.T.astype(jnp.float32), left_side=True, lower=True
    )
    quad = jnp.sum(solved * solved, axis=0) / width
    influence = lax.psum(quad, "layer")
    return (lower.T[None], mine[None], influence)


def solution(mesh):
    placed = (
        P("layer", "rep", None),
        P("layer", "rep", None),
        P("layer", None, None),
        P("layer", None, None),
        P("rep"),
        P("rep"),
    )
    return jax.shard_map(
        on_device,
        mesh=mesh,
        in_specs=placed,
        out_specs=(P("layer", None, None), P("layer", "rep", None), P("rep")),
        check_vma=False,
    )
```

profile of v0, /device:TPU:1, one launch (start us, length us, event | category | flops | bytes accessed | tf_op | source)
XLA Modules:
  0.0 520.8 jit_solution(4648112741380501496)
XLA Ops:
  7.2 0.9 convert_reduce_fusion
  8.1 3.3 collective-permute-start.1
  11.5 0.8 compare_convert_fusion
  12.3 6.2 %fusion.10 = bf16[32,512]{1,0:T(8,128)(2,1)S(1)} fusion(bf16[1,512,8192]{2,1,0:T(8,128)(2,1)} %param.6, bf16[1,32,8192]{2,1,0:T(8,128)(2,1)} %param.8), kind=kOutput, calls=%fused_computation.33 | convolution fusion | flops 268451840 | bytes 8945664 | tf_op jit(solution)/shard_map/dot_general | solution.py:20
  18.5 6.7 %fusion.7 = f32[63,32,32]{2,1,0:T(8,128)S(1)} fusion(bf16[32,512]{1,0:T(8,128)(2,1)S(1)} %fusion.10, bf16[63,512]{1,0:T(8,128)(2,1)S(1)} %compare_convert_fusion, bf16[1,512,8192]{2,1,0:T(8,128)(2,1)} %param.7, bf16[1,32,8192]{2,1,0:T(8,128)(2,1)S(1)} %copy-done), kind=kOutput, calls=%fused_computation.14 | convolution fusion | flops 335544320 | bytes 9268224 | tf_op jit(solution)/shard_map/dot_general | solution.py:31
  25.2 1.9 collective-permute-start
  29.3 1.4 maximum_sqrt_fusion
  31.1 3.7 collective-permute-start.3
  35.0 1.9 collective-permute-start.2
  37.1 3.5 collective-permute-done.2
  40.6 2.8 fusion.102
  43.4 118.1 %all-reduce.3.cloned.1.call-done = f32[1024,1024]{0,1:T(8,128)} async-done(((f32[1024,1024]{0,1:T(8,128)}), f32[1024,1024]{0,1:T(8,128)}) %all-reduce.3.cloned.1.call-update) | async-done | bytes 4194320 | tf_op jit(solution)/shard_map/psum | solution.py:65
  161.5 5.1 select_add_fusion
  166.6 5.5 %copy.29 = f32[1024,1024]{1,0:T(8,128)} copy(f32[1024,1024]{0,1:T(8,128)} %select_add_fusion) | data formatting | bytes 8388608 | tf_op jit(solution)/shard_map/add | solution.py:67
  172.1 4.5 fusion.4
  176.6 2.0 copy-done.2
  178.6 11.7 %cholesky.222 = f32[128,128]{1,0:T(8,128)S(1)} custom-call(f32[128,128]{1,0:T(8,128)S(1)} %cholesky.577), custom_call_target="Cholesky" | custom-call | tf_op jit(solution)/shard_map/jit(cholesky)/cholesky | solution.py:68
  190.4 9.8 %custom-call.62 = f32[1,128,128]{1,2,0:T(8,128)S(1)} custom-call(f32[1,128,128]{2,1,0:T(8,128)S(1)} %get-tuple-element.48), custom_call_target="InvertDiagBlocksLowerTriangular" | custom-call | tf_op jit(solution)/shard_map/jit(cholesky)/cholesky | solution.py:68
  200.3 1.5 fusion.35
  202.0 1.6 convolution_subtract_fusion
  203.6 11.7 %cholesky.243 = f32[128,128]{1,0:T(8,128)S(1)} custom-call(f32[128,128]{1,0:T(8,128)S(1)} %cholesky.581), custom_call_target="Cholesky" | custom-call | tf_op jit(solution)/shard_map/jit(cholesky)/cholesky | solution.py:68
  215.6 9.8 %custom-call.63 = f32[1,128,128]{1,2,0:T(8,128)S(1)} custom-call(f32[1,128,128]{2,1,0:T(8,128)S(1)} %get-tuple-element.46), custom_call_target="InvertDiagBlocksLowerTriangular" | custom-call | tf_op jit(solution)/shard_map/jit(cholesky)/cholesky | solution.py:68
  226.6 2.0 copy-done.1
  228.5 2.4 convolution_subtract_fusion.1
  230.9 11.7 %cholesky.466 = f32[128,128]{1,0:T(8,128)S(1)} custom-call(f32[128,128]{1,0:T(8,128)S(1)} %cholesky.586), custom_call_target="Cholesky" | custom-call | tf_op jit(solution)/shard_map/jit(cholesky)/cholesky | solution.py:68
  243.4 9.8 %custom-call.64 = f32[1,128,128]{1,2,0:T(8,128)S(1)} custom-call(f32[1,128,128]{2,1,0:T(8,128)S(1)} %get-tuple-element.44), custom_call_target="InvertDiagBlocksLowerTriangular" | custom-call | tf_op jit(solution)/shard_map/jit(cholesky)/cholesky | solution.py:68
  253.2 1.3 convolution_dynamic-update-slice_fusion.1
  254.5 3.5 convolution_subtract_fusion.2
  258.1 11.7 %cholesky.485 = f32[128,128]{1,0:T(8,128)S(1)} custom-call(f32[128,128]{1,0:T(8,128)S(1)} %cholesky.591), custom_call_target="Cholesky" | custom-call | tf_op jit(solution)/shard_map/jit(cholesky)/cholesky | solution.py:68
  270.5 9.8 %custom-call.65 = f32[1,128,128]{1,2,0:T(8,128)S(1)} custom-call(f32[1,128,128]{2,1,0:T(8,128)S(1)} %get-tuple-element.42), custom_call_target="InvertDiagBlocksLowerTriangular" | custom-call | tf_op jit(solution)/shard_map/jit(cholesky)/cholesky | solution.py:68
  280.4 1.1 convolution_dynamic-update-slice_fusion.2
  281.5 3.2 convolution_subtract_fusion.3
  284.7 11.9 %cholesky.504 = f32[128,128]{1,0:T(8,128)S(1)} custom-call(f32[128,128]{1,0:T(8,128)S(1)} %cholesky.596), custom_call_target="Cholesky" | custom-call | tf_op jit(solution)/shard_map/jit(cholesky)/cholesky | solution.py:68
  297.3 9.8 %custom-call.66 = f32[1,128,128]{1,2,0:T(8,128)S(1)} custom-call(f32[1,128,128]{2,1,0:T(8,128)S(1)} %get-tuple-element.40), custom_call_target="InvertDiagBlocksLowerTriangular" | custom-call | tf_op jit(solution)/shard_map/jit(cholesky)/cholesky | solution.py:68
  307.1 1.1 convolution_dynamic-update-slice_fusion.3
  308.2 3.1 convolution_subtract_fusion.4
  311.3 11.7 %cholesky.524 = f32[128,128]{1,0:T(8,128)S(1)} custom-call(f32[128,128]{1,0:T(8,128)S(1)} %cholesky.601), custom_call_target="Cholesky" | custom-call | tf_op jit(solution)/shard_map/jit(cholesky)/cholesky | solution.py:68
  323.8 9.8 %custom-call.67 = f32[1,128,128]{1,2,0:T(8,128)S(1)} custom-call(f32[1,128,128]{2,1,0:T(8,128)S(1)} %get-tuple-element.38), custom_call_target="InvertDiagBlocksLowerTriangular" | custom-call | tf_op jit(solution)/shard_map/jit(cholesky)/cholesky | solution.py:68
  333.6 1.0 convolution_dynamic-update-slice_fusion.4
  334.6 2.9 convolution_subtract_fusion.5
  337.5 11.7 %cholesky.544 = f32[128,128]{1,0:T(8,128)S(1)} custom-call(f32[128,128]{1,0:T(8,128)S(1)} %cholesky.606), custom_call_target="Cholesky" | custom-call | tf_op jit(solution)/shard_map/jit(cholesky)/cholesky | solution.py:68
  350.0 9.8 %custom-call.68 = f32[1,128,128]{1,2,0:T(8,128)S(1)} custom-call(f32[1,128,128]{2,1,0:T(8,128)S(1)} %get-tuple-element.36), custom_call_target="InvertDiagBlocksLowerTriangular" | custom-call | tf_op jit(solution)/shard_map/jit(cholesky)/cholesky | solution.py:68
  359.8 0.9 convolution_dynamic-update-slice_fusion.5
  360.7 2.1 convolution_subtract_fusion.6
  362.8 11.7 %cholesky.562 = f32[128,128]{1,0:T(8,128)S(1)} custom-call(f32[128,128]{1,0:T(8,128)S(1)} %convolution_subtract_fusion.6), custom_call_target="Cholesky" | custom-call | tf_op jit(solution)/shard_map/jit(cholesky)/cholesky | solution.py:68
  385.0 6.7 %fusion.5 = (f32[1024,1024]{0,1:T(8,128)}, f32[1,1024,1024]{2,1,0:T(8,128)}) fusion(f32[1024,1024]{0,1:T(8,128)} %constant_dynamic-update-slice_fusion.30, pred[]{:T(512)S(6)} %cholesky.576), kind=kLoop, calls=%fused_computation.12 | loop fusion | flops 4194304 | bytes 12582913 | tf_op jit(solution)/shard_map/triangular_solve | solution.py:69
  391.7 24.1 %while.1 = (s32[]{:T(128)}, f32[1024,1024]{0,1:T(8,128)}, s32[8,2]{0,1:T(2,128)S(1)}, f32[8,128,128]{2,1,0:T(8,128)S(1)}, s32[]{:T(128)}) while((s32[]{:T(128)}, f32[1024,1024]{0,1:T(8,128)}, s32[8,2]{0,1:T(2,128)S(1)}, f32[8,128,128]{2,1,0:T(8,128)S(1)}, s32[]{:T(128)}) %tuple.59), condition=%wide.while_cond, body=%wide.while_body.sunk | while | flops 2 | bytes 393329 | solution.py:69
  392.6 2.3 dynamic-slice.7
  395.5 2.3 dynamic-slice.7
  398.5 2.3 dynamic-slice.7
  401.5 2.3 dynamic-slice.7
  404.5 2.3 dynamic-slice.7
  407.5 2.3 dynamic-slice.7
  410.5 2.3 dynamic-slice.7
  413.5 2.2 dynamic-slice.7
  415.9 78.6 %custom-call.69 = f32[8,128,128]{1,2,0:T(8,128)S(1)} custom-call(f32[8,128,128]{2,1,0:T(8,128)S(1)} %get-tuple-element.10), custom_call_target="InvertDiagBlocksLowerTriangular" | custom-call | tf_op jit(solution)/shard_map/triangular_solve | solution.py:69
  494.6 1.0 convolution_subtract_fusion.10
  495.8 1.1 convolution_subtract_fusion.9
  497.1 1.2 convolution_subtract_fusion.8
  498.5 1.2 convolution_subtract_fusion.7
  499.9 1.3 convolution_subtract_fusion.13
  501.3 1.3 convolution_subtract_fusion.12
  502.8 1.4 convolution_subtract_fusion.11
  504.6 9.0 %psum.15 = f32[32]{0:T(128)} all-reduce(f32[32]{0:T(128)S(1)} %broadcast_multiply_fusion), channel_id=1, replica_groups=mesh['rep'=32,'layer'=4] {'layer'}, use_global_device_ids=true, to_apply=%region_20.21 | all-reduce | flops 32 | bytes 256 | tf_op jit(solution)/shard_map/psum | solution.py:73
  (116 shorter events, 21.1 us)
Async XLA Ops:
  7.2 11.3 %copy-start = (bf16[1,32,8192]{2,1,0:T(8,128)(2,1)S(1)}, bf16[1,32,8192]{2,1,0:T(8,128)(2,1)}, u32[]{:S(2)}) copy-start(bf16[1,32,8192]{2,1,0:T(8,128)(2,1)} %param.9) | copy-start | bytes 1572868
  7.2 154.4 %all-reduce.3.cloned.1.call-start = ((), (), s32[]{:S(2)}) async-start(), calls=%async_computation | async-start | bytes 8388608 | tf_op jit(solution)/shard_map/psum | solution.py:65
  8.1 21.2 %collective-permute-start.1 = (f32[1]{0:T(128)S(1)}, f32[1]{0:T(128)}, u32[]{:S(2)}, u32[]{:S(2)}) collective-permute-start(f32[1]{0:T(128)S(1)} %bitcast.148), channel_id=1, source_target_pairs={{4,0},{8,4},{12,8},{16,12},{20,16},{24,20},{28,24},{32,28},{36,32}... | collective-permute-start | bytes 20 | tf_op jit(solution)/shard_map/ppermute | solution.py:15
  18.4 9.5 %copy-start.4 = (s32[512]{0:T(512)S(1)}, s32[512]{0:T(512)}, u32[]{:S(2)}) copy-start(s32[512]{0:T(512)} %param.10) | copy-start | bytes 6148
  18.5 10.8 %copy-start.5 = (s32[62]{0:T(128)S(1)}, s32[62]{0:T(128)}, u32[]{:S(2)}) copy-start(s32[62]{0:T(128)} %param.11) | copy-start | bytes 748
  25.2 5.5 %collective-permute-start = (f32[1,1024]{1,0:T(1,128)S(1)}, f32[1,1024]{1,0:T(1,128)S(1)}, u32[]{:S(2)}, u32[]{:S(2)}) collective-permute-start(f32[1,1024]{1,0:T(1,128)S(1)} %slice.248), channel_id=1, source_target_pairs={{4,0},{8,4},{12,8},{16,12},{20,16},{24,20},{28,24},{32,28},{36,32}... | collective-permute-start | bytes 12296 | tf_op jit(solution)/shard_map/ppermute | solution.py:15
  31.1 6.0 %collective-permute-start.3 = (bf16[32,1024]{1,0:T(8,128)(2,1)S(1)}, bf16[32,1024]{1,0:T(8,128)(2,1)S(1)}, u32[]{:S(2)}, u32[]{:S(2)}) collective-permute-start(bf16[32,1024]{1,0:T(8,128)(2,1)S(1)} %convolution_convert_fusion), channel_id=1, source_target_pairs={{0,4},{4,8},{8,12},{12,16},{16,20},{20,24},{24,28},{28,32},{32,36}... | collective-permute-start | bytes 196616 | tf_op jit(solution)/shard_map/ppermute | solution.py:15
  35.0 5.6 %collective-permute-start.2 = (bf16[32,1024]{1,0:T(8,128)(2,1)S(1)}, bf16[32,1024]{1,0:T(8,128)(2,1)S(1)}, u32[]{:S(2)}, u32[]{:S(2)}) collective-permute-start(bf16[32,1024]{1,0:T(8,128)(2,1)S(1)} %convolution_convert_fusion.1), channel_id=1, source_target_pairs={{4,0},{8,4},{12,8},{16,12},{20,16},{24,20},{28,24},{32,28},{36,32}... | collective-permute-start | bytes 196616 | tf_op jit(solution)/shard_map/ppermute | solution.py:15
  40.6 453.8 %copy-start.3 = (bf16[32,1024]{1,0:T(8,128)(2,1)}, bf16[32,1024]{1,0:T(8,128)(2,1)S(1)}, u32[]{:S(2)}) copy-start(bf16[32,1024]{1,0:T(8,128)(2,1)S(1)} %get-tuple-element.28) | copy-start | bytes 196612
  176.6 2.0 copy-start.2
  226.5 2.0 copy-start.1
Sparse Core Ops, SparseCore 0:
  43.5 117.9 all-reduce.2
where the time goes:
time: 530 us; the launch traced here: 521 us
  other arithmetic  267 us (50%)
  waiting for transfers between devices  122 us (23%)
  matrix products  52.1 us (10%)
  local copies, waits for them, and re-layouts  39.6 us (7%)
  between operations  20.2 us (4%)
  starting transfers between devices  10.9 us (2%)
  blocking collectives  8.97 us (2%)
    another operation x30, other arithmetic, on_device(): lower = jnp.linalg.cholesky(hessian)  167 us
    psum x1, waiting for transfers between devices, on_device(): gram = lax.psum(local_gram, 'rep')  118 us
    another operation x3, other arithmetic, on_device(): lax.linalg.triangular_solve(lower, mine.T.astype(jnp.float32), left_side=...  85.3 us
    another operation x14, matrix products, on_device(): lower = jnp.linalg.cholesky(hessian)  26.2 us
    another operation x40, local copies, waits for them, and re-layouts  23.6 us
    ppermute x4, starting transfers between devices, shifted(): return lax.ppermute(block, axis, route)  10.8 us
  transfers between devices with their start and end apart: 5, of which 2 were waited for; matrix products, arithmetic and copies ran while one was open for 3% of the time, Pallas kernels for 0%

commit v1 on v0

--- a/solution.py
+++ b/solution.py
@@ -1,12 +1,124 @@
+import functools
+
 import jax
 import jax.numpy as jnp
 from jax import lax
+from jax.experimental import pallas as pl
+from jax.experimental.pallas import tpu as pltpu
 from jax.sharding import PartitionSpec as P
 
 BAL = 32
+B = 128
+S = 32
+DAMPING = 0.05
+F32=jnp.float32; BF=jnp.bfloat16
 
+def split(x):
+    hi = x.astype(BF)
+    lo = (x - hi.astype(F32)).astype(BF)
+    return hi, lo
 
-DAMPING = 0.05
+def dotT(a, b):
+    return lax.dot_general(a, b, (((0,),(0,)),((),())), preferred_element_type=F32)
+def dot(a, b):
+    return lax.dot_general(a, b, (((1,),(0,)),((),())), preferred_element_type=F32)
+
+def chol_rows(D, V, W):
+    nb = S//8
+    row = lax.broadcasted_iota(jnp.int32,(8,128),0)
+    C = [[None]*nb for _ in range(S)]
+    for j in range(S):
+        for i in range(j//8, nb):
+            C[j][i] = jnp.broadcast_to(D[8*i:8*i+8, j:j+1], (8,128))
+    Vr = [[V[8*i:8*i+8, 128*c:128*c+128] for c in range(W//128)] for i in range(nb)]
+    dv = [jnp.ones((8,128),F32) for _ in range(nb)]
+    for j in range(S):
+        jb, js = divmod(j,8)
+        u = C[j]
+        piv = jnp.broadcast_to(u[jb][js:js+1], (8,128))
+        r = 1.0/piv
+        dv[jb] = jnp.where(row==js, piv, dv[jb])
+        w = [None]*nb
+        for i in range(jb, nb): w[i] = u[i]*r
+        for j2 in range(j+1, S):
+            q = jnp.broadcast_to(u[j2//8][j2%8:j2%8+1], (8,128))
+            for i in range(j2//8, nb):
+                C[j2][i] = C[j2][i] - w[i]*q
+        for c in range(W//128):
+            vrow = jnp.broadcast_to(Vr[jb][c][js:js+1], (8,128))
+            for i in range(jb, nb):
+                if i==jb:
+                    if js==7: continue
+                    wi = jnp.where(row>js, w[i], 0.0)
+                else: wi = w[i]
+                Vr[i][c] = Vr[i][c] - wi*vrow
+    out=[]
+    for i in range(nb):
+        s = lax.rsqrt(dv[i])
+        out.append(jnp.concatenate([Vr[i][c]*s for c in range(W//128)], axis=1))
+    return jnp.concatenate(out, axis=0)
+
+def factor_diag(A):
+    r_ = lax.broadcasted_iota(jnp.int32,(B,B),0); c_=lax.broadcasted_iota(jnp.int32,(B,B),1)
+    eye = jnp.where(r_==c_, 1.0, 0.0).astype(F32)
+    V = jnp.concatenate([A, eye], axis=1)
+    rows=[]
+    for s in range(B//S):
+        P = chol_rows(V[:S, s*S:s*S+S], V[:S], 2*B)
+        rows.append(P)
+        if s < B//S-1:
+            h,l = split(P)
+            K = jnp.concatenate([h,h,l],axis=0)[:, (s+1)*S:B]
+            Q = jnp.concatenate([h,l,h],axis=0)
+            V = V[S:] - dotT(K,Q)
+    Z = jnp.concatenate(rows,axis=0)
+    return Z[:, :B], Z[:, B:]
+
+def k3_kernel(n, f_ref, mine_ref, fac_ref, q_ref, rh, rl):
+    docs = f_ref.shape[0]
+    W = n + 128
+    nb = n//B
+    ri = lax.broadcasted_iota(jnp.int32,(B,B),0); ci=lax.broadcasted_iota(jnp.int32,(B,B),1)
+    acc = jnp.zeros((1,128),F32)
+    for k in range(nb):
+        c0 = k*B
+        fk = f_ref[:, c0:c0+B]
+        H = dotT(fk, f_ref[:, c0:n])*(1.0/docs)
+        mk = mine_ref[:, c0:c0+B].astype(F32).T
+        X = jnp.concatenate([mk, jnp.zeros((B,128-mk.shape[1]),F32)],axis=1)
+        Srow = jnp.concatenate([H, X],axis=1)
+        if k>0:
+            lh = rh[:c0, c0:c0+B]; ll = rl[:c0, c0:c0+B]
+            gh = rh[:c0, c0:W]; gl = rl[:c0, c0:W]
+            Srow = Srow - (dotT(lh, gh) + dotT(lh, gl) + dotT(ll, gh))
+        A = Srow[:, :B] + jnp.where(ri==ci, DAMPING, 0.0)
+        R, T = factor_diag(A)
+        R = jnp.where(ci>=ri, R, 0.0)
+        th, tl = split(T)
+        sh, sl = split(Srow[:, B:])
+        Pn = dot(th, sh) + dot(th, sl) + dot(tl, sh)
+        fac_ref[c0:c0+B, c0:c0+B] = R
+        if k < nb-1:
+            fac_ref[c0:c0+B, c0+B:n] = Pn[:, :n-c0-B]
+            ph, pl_ = split(Pn)
+            rh[c0:c0+B, c0+B:W] = ph
+            rl[c0:c0+B, c0+B:W] = pl_
+        if k>0:
+            fac_ref[c0:c0+B, 0:c0] = jnp.zeros((B,c0),F32)
+        sol = Pn[:, n-c0-B:]
+        acc = acc + jnp.sum(sol*sol, axis=0, keepdims=True)
+    q_ref[...] = jnp.broadcast_to(acc, (8,128))
+
+def k3(f, mine):
+    docs, n = f.shape
+    return pl.pallas_call(
+        functools.partial(k3_kernel, n),
+        out_shape=(jax.ShapeDtypeStruct((n,n),F32), jax.ShapeDtypeStruct((8,128),F32)),
+        in_specs=[pl.BlockSpec(memory_space=pltpu.VMEM)]*2,
+        out_specs=(pl.BlockSpec(memory_space=pltpu.VMEM),)*2,
+        scratch_shapes=[pltpu.VMEM((n,n+128),BF), pltpu.VMEM((n,n+128),BF)],
+        compiler_params=pltpu.CompilerParams(vmem_limit_bytes=48*2**20),
+    )(f, mine)
 
 
 def shifted(block, axis, distance):
@@ -60,18 +172,11 @@
     mine = (
         staying.astype(jnp.float32) + from_right.astype(jnp.float32) + from_left.astype(jnp.float32)
     ).astype(jnp.bfloat16)
-    rows_contract = (((0,), (0,)), ((), ()))
-    local_gram = lax.dot_general(mine, mine, rows_contract, preferred_element_type=jnp.float32)
-    gram = lax.psum(local_gram, "rep")
-    total_docs = BAL * n_rep
-    hessian = gram / total_docs + DAMPING * jnp.eye(width, dtype=jnp.float32)
-    lower = jnp.linalg.cholesky(hessian)
-    solved = lax.linalg.triangular_solve(
-        lower, mine.T.astype(jnp.float32), left_side=True, lower=True
-    )
-    quad = jnp.sum(solved * solved, axis=0) / width
+    everyone = lax.all_gather(mine, "rep", axis=0, tiled=True)
+    factor, quad = k3(everyone, mine)
+    quad = quad[0, :BAL] / width
     influence = lax.psum(quad, "layer")
-    return (lower.T[None], mine[None], influence)
+    return (factor[None], mine[None], influence)
 
 
 def solution(mesh):

time: 530 us -> 144 us (0.27); the launches traced: 521 us -> 142 us
  other arithmetic: 267 us -> 5.34 us
  waiting for transfers between devices: 122 us -> 52.2 us
  matrix products: 52.1 us -> 13.4 us
  local copies, waits for them, and re-layouts: 39.6 us -> 3.3 us
  Pallas kernels: 0 us -> 33.9 us
  between operations: 20.2 us -> 14.2 us
    another operation x33 -> x0, other arithmetic: 253 us -> none  [the longest x30 167 us: on_device(): lower = jnp.linalg.cholesky(hessian)]
    psum x1 -> x0, waiting for transfers between devices: 118 us -> none  [on_device(): gram = lax.psum(local_gram, 'rep')]
    all_gather x0 -> x1, waiting for transfers between devices: none -> 51.2 us  [on_device(): everyone = lax.all_gather(mine, 'rep', axis=0, tiled=True)]
    another operation x29 -> x0, matrix products: 36 us -> none  [the longest x14 26.2 us: on_device(): lower = jnp.linalg.cholesky(hessian)]
    pallas_call x0 -> x1, Pallas kernels: none -> 33.9 us  [k3(): pl.pallas_call(functools.partial(k3_kernel, n), out_shape=(jax.ShapeDtype...]
    another operation x66 -> x0, local copies, waits for them, and re-layouts: 29.2 us -> none
    add x1 -> x0, local copies, waits for them, and re-layouts: 5.49 us -> none  [on_device(): hessian = gram / total_docs + DAMPING * jnp.eye(width, dtype=jnp.float32)]
  transfers between devices with their start and end apart: 5 -> 5, of which waited for: 2 -> 2; matrix products, arithmetic and copies ran while one was open for 3% -> 12% of each run, Pallas kernels for 0% -> 0%
where the time goes in v1:
time: 144 us; the launch traced here: 142 us
  waiting for transfers between devices  52.2 us (36%)
  Pallas kernels  33.9 us (24%)
  between operations  14.2 us (10%)
  matrix products  13.4 us (9%)
  starting transfers between devices  11 us (8%)
  blocking collectives  8.92 us (6%)
  other arithmetic  5.34 us (4%)
  local copies, waits for them, and re-layouts  3.3 us (2%)
    all_gather x1, waiting for transfers between devices, on_device(): everyone = lax.all_gather(mine, 'rep', axis=0, tiled=True)  51.2 us
    pallas_call x1, Pallas kernels, k3(): pl.pallas_call(functools.partial(k3_kernel, n), out_shape=(jax.ShapeDtype...  33.9 us
    ppermute x4, starting transfers between devices, shifted(): return lax.ppermute(block, axis, route)  11 us
    psum x1, blocking collectives, on_device(): influence = lax.psum(quad, 'layer')  8.92 us
    dot_general x1, matrix products, on_device(): lax.dot_general(masked, right, (((2,), (1,)), ((), ())), preferred_elemen...  6.67 us
    dot_general x1, matrix products, on_device(): lax.dot_general(in_projection[0], activations[0], contract, preferred_ele...  6.17 us
  transfers between devices with their start and end apart: 5, of which 2 were waited for; matrix products, arithmetic and copies ran while one was open for 12% of the time, Pallas kernels for 0%

profile of v1, /device:TPU:1, one launch (start us, length us, event | category | flops | bytes accessed | tf_op | source)
XLA Modules:
  0.0 142.3 jit_solution(14543277174832901497)
XLA Ops:
  7.2 0.0 copy-start
  7.2 0.0 all-gather.2.cloned.1.call-start
  7.2 0.9 convert_reduce_fusion
  8.1 3.3 %collective-permute-start.1 = (f32[1]{0:T(128)S(1)}, f32[1]{0:T(128)}, u32[]{:S(2)}, u32[]{:S(2)}) collective-permute-start(f32[1]{0:T(128)S(1)} %bitcast.43), channel_id=1, source_target_pairs={{4,0},{8,4},{12,8},{16,12},{20,16},{24,20},{28,24},{32,28},{36,32}... | collective-permute-start | bytes 20 | tf_op jit(solution)/shard_map/ppermute | solution.py:127
  11.5 0.8 compare_convert_fusion
  12.3 0.0 copy-start.3
  12.3 0.0 copy-start.4
  12.3 6.2 %fusion.7 = bf16[32,512]{1,0:T(8,128)(2,1)S(1)} fusion(bf16[1,512,8192]{2,1,0:T(8,128)(2,1)} %param.6, bf16[1,32,8192]{2,1,0:T(8,128)(2,1)} %param.8), kind=kOutput, calls=%fused_computation.10 | convolution fusion | flops 268451840 | bytes 8945664 | tf_op jit(solution)/shard_map/dot_general | solution.py:132
  18.5 0.0 copy-done
  18.5 6.7 %fusion.4 = f32[63,32,32]{2,1,0:T(8,128)S(1)} fusion(bf16[32,512]{1,0:T(8,128)(2,1)S(1)} %fusion.7, bf16[63,512]{1,0:T(8,128)(2,1)S(1)} %compare_convert_fusion, bf16[1,512,8192]{2,1,0:T(8,128)(2,1)} %param.7, bf16[1,32,8192]{2,1,0:T(8,128)(2,1)S(1)} %copy-done), kind=kOutput, calls=%fused_computation.4 | convolution fusion | flops 335544320 | bytes 9268224 | tf_op jit(solution)/shard_map/dot_general | solution.py:143
  25.2 0.1 slice.28
  25.2 1.9 %collective-permute-start = (f32[1,1024]{1,0:T(1,128)S(1)}, f32[1,1024]{1,0:T(1,128)S(1)}, u32[]{:S(2)}, u32[]{:S(2)}) collective-permute-start(f32[1,1024]{1,0:T(1,128)S(1)} %slice.28), channel_id=1, source_target_pairs={{4,0},{8,4},{12,8},{16,12},{20,16},{24,20},{28,24},{32,28},{36,32}... | collective-permute-start | bytes 12296 | tf_op jit(solution)/shard_map/ppermute | solution.py:127
  27.2 0.1 slice.32
  27.2 0.0 copy-done.3
  27.3 0.6 reduce_max.9
  27.9 0.0 copy-done.4
  27.9 0.7 compare_convert_fusion.1
  28.6 0.7 copy.9
  29.3 0.0 collective-permute-done.1
  29.3 1.4 maximum_sqrt_fusion
  30.8 0.0 collective-permute-done
  30.8 0.2 fusion.21
  31.0 0.2 convolution_convert_fusion
  31.1 0.2 convolution_convert_fusion.1
  31.3 1.9 %collective-permute-start.2 = (bf16[32,1024]{1,0:T(8,128)(2,1)S(1)}, bf16[32,1024]{1,0:T(8,128)(2,1)S(1)}, u32[]{:S(2)}, u32[]{:S(2)}) collective-permute-start(bf16[32,1024]{1,0:T(8,128)(2,1)S(1)} %convolution_convert_fusion.1), channel_id=1, source_target_pairs={{4,0},{8,4},{12,8},{16,12},{20,16},{24,20},{28,24},{32,28},{36,32}... | collective-permute-start | bytes 196616 | tf_op jit(solution)/shard_map/ppermute | solution.py:127
  33.3 3.8 %collective-permute-start.3 = (bf16[32,1024]{1,0:T(8,128)(2,1)S(1)}, bf16[32,1024]{1,0:T(8,128)(2,1)S(1)}, u32[]{:S(2)}, u32[]{:S(2)}) collective-permute-start(bf16[32,1024]{1,0:T(8,128)(2,1)S(1)} %convolution_convert_fusion), channel_id=1, source_target_pairs={{0,4},{4,8},{8,12},{12,16},{16,20},{20,24},{24,28},{28,32},{32,36}... | collective-permute-start | bytes 196616 | tf_op jit(solution)/shard_map/ppermute | solution.py:127
  37.1 0.2 fusion.6
  37.3 0.0 collective-permute-done.2
  37.3 0.9 collective-permute-done.3
  38.3 0.7 add_convert_fusion.mine_ref
  38.9 0.0 all-gather.2.cloned.1.call-update
  38.9 51.2 %all-gather.2.cloned.1.call-done.f_ref = bf16[1024,1024]{1,0:T(8,128)(2,1)} async-done(((bf16[32,1024]{1,0:T(8,128)(2,1)}), bf16[1024,1024]{1,0:T(8,128)(2,1)}) %all-gather.2.cloned.1.call-update) | async-done | bytes 2097168 | tf_op jit(solution)/shard_map/all_gather | solution.py:175
  90.2 0.0 copy-start.1
  90.2 1.6 %copy-done.1 = bf16[1024,1024]{1,0:T(8,128)(2,1)S(1)} copy-done((bf16[1024,1024]{1,0:T(8,128)(2,1)S(1)}, bf16[1024,1024]{1,0:T(8,128)(2,1)}, u32[]{:S(2)}) %copy-start.1) | copy-done | bytes 2097176
  91.8 0.0 copy-start.2
  91.8 0.8 copy-done.2
  92.6 33.9 %shard_map.85 = (f32[1024,1024]{1,0:T(8,128)}, f32[8,128]{1,0:T(8,128)S(1)}) custom-call(bf16[1024,1024]{1,0:T(8,128)(2,1)S(1)} %copy-done.1, bf16[32,1024]{1,0:T(8,128)(2,1)S(1)} %copy-done.2), custom_call_target="tpu_custom_call" | custom-call | tf_op jit(solution)/shard_map/pallas_call | solution.py:114
  126.5 8.9 %psum.7 = f32[32]{0:T(128)} all-reduce(f32[32]{0:T(128)S(1)} %multiply_bitcast_fusion), channel_id=1, replica_groups=mesh['rep'=32,'layer'=4] {'layer'}, use_global_device_ids=true, to_apply=%region_2.3 | all-reduce | flops 32 | bytes 256 | tf_op jit(solution)/shard_map/psum | solution.py:178
  (6 shorter events, 0.0 us)
Async XLA Ops:
  7.2 11.3 %copy-start = (bf16[1,32,8192]{2,1,0:T(8,128)(2,1)S(1)}, bf16[1,32,8192]{2,1,0:T(8,128)(2,1)}, u32[]{:S(2)}) copy-start(bf16[1,32,8192]{2,1,0:T(8,128)(2,1)} %param.9) | copy-start | bytes 1572868
  7.2 83.0 %all-gather.2.cloned.1.call-start = ((), (), s32[]{:S(2)}) async-start(), calls=%async_computation | async-start | bytes 2162688 | tf_op jit(solution)/shard_map/all_gather | solution.py:175
  8.1 21.2 %collective-permute-start.1 = (f32[1]{0:T(128)S(1)}, f32[1]{0:T(128)}, u32[]{:S(2)}, u32[]{:S(2)}) collective-permute-start(f32[1]{0:T(128)S(1)} %bitcast.43), channel_id=1, source_target_pairs={{4,0},{8,4},{12,8},{16,12},{20,16},{24,20},{28,24},{32,28},{36,32}... | collective-permute-start | bytes 20 | tf_op jit(solution)/shard_map/ppermute | solution.py:127
  12.3 15.0 %copy-start.3 = (s32[512]{0:T(512)S(1)}, s32[512]{0:T(512)}, u32[]{:S(2)}) copy-start(s32[512]{0:T(512)} %param.10) | copy-start | bytes 6148
  12.3 15.6 %copy-start.4 = (s32[62]{0:T(128)S(1)}, s32[62]{0:T(128)}, u32[]{:S(2)}) copy-start(s32[62]{0:T(128)} %param.11) | copy-start | bytes 748
  25.2 5.5 %collective-permute-start = (f32[1,1024]{1,0:T(1,128)S(1)}, f32[1,1024]{1,0:T(1,128)S(1)}, u32[]{:S(2)}, u32[]{:S(2)}) collective-permute-start(f32[1,1024]{1,0:T(1,128)S(1)} %slice.28), channel_id=1, source_target_pairs={{4,0},{8,4},{12,8},{16,12},{20,16},{24,20},{28,24},{32,28},{36,32}... | collective-permute-start | bytes 12296 | tf_op jit(solution)/shard_map/ppermute | solution.py:127
  31.3 6.0 %collective-permute-start.2 = (bf16[32,1024]{1,0:T(8,128)(2,1)S(1)}, bf16[32,1024]{1,0:T(8,128)(2,1)S(1)}, u32[]{:S(2)}, u32[]{:S(2)}) collective-permute-start(bf16[32,1024]{1,0:T(8,128)(2,1)S(1)} %convolution_convert_fusion.1), channel_id=1, source_target_pairs={{4,0},{8,4},{12,8},{16,12},{20,16},{24,20},{28,24},{32,28},{36,32}... | collective-permute-start | bytes 196616 | tf_op jit(solution)/shard_map/ppermute | solution.py:127
  33.3 5.0 %collective-permute-start.3 = (bf16[32,1024]{1,0:T(8,128)(2,1)S(1)}, bf16[32,1024]{1,0:T(8,128)(2,1)S(1)}, u32[]{:S(2)}, u32[]{:S(2)}) collective-permute-start(bf16[32,1024]{1,0:T(8,128)(2,1)S(1)} %convolution_convert_fusion), channel_id=1, source_target_pairs={{0,4},{4,8},{8,12},{12,16},{16,20},{20,24},{24,28},{28,32},{32,36}... | collective-permute-start | bytes 196616 | tf_op jit(solution)/shard_map/ppermute | solution.py:127
  90.2 1.6 %copy-start.1 = (bf16[1024,1024]{1,0:T(8,128)(2,1)S(1)}, bf16[1024,1024]{1,0:T(8,128)(2,1)}, u32[]{:S(2)}) copy-start(bf16[1024,1024]{1,0:T(8,128)(2,1)} %all-gather.2.cloned.1.call-done.f_ref) | copy-start | bytes 6291460
  91.8 0.8 copy-start.2
Sparse Core Ops, SparseCore 0:
  39.1 51.0 all-gather.1

commit v2 on v0

v2 whole, which is shorter than its diff:
```python
import functools

import jax
import jax.numpy as jnp
from jax import lax
from jax.experimental import pallas as pl
from jax.experimental.pallas import tpu as pltpu
from jax.sharding import PartitionSpec

BAL = 32
BLOCK = 128
GROUP = 32
DAMPING = 0.05
TOK = 128
F32 = jnp.float32
BF16 = jnp.bfloat16
VMEM = pl.BlockSpec(memory_space=pltpu.VMEM)


def split(x):
    hi = x.astype(BF16)
    lo = (x - hi.astype(F32)).astype(BF16)
    return hi, lo


def dot_t(a, b):
    return lax.dot_general(a, b, (((0,), (0,)), ((), ())), preferred_element_type=F32)


def dot(a, b):
    return lax.dot_general(a, b, (((1,), (0,)), ((), ())), preferred_element_type=F32)


def iota(shape, axis):
    return lax.broadcasted_iota(jnp.int32, shape, axis)


def onehot(mask, dtype=BF16):
    return jnp.where(mask, 1.0, 0.0).astype(dtype)


def front_kernel(
    steps_k, acts_ref, grads_ref, in_ref, out_ref, segs_ref, moves_ref,
    arr_ref, aux_ref, left_acc, right_acc, sums, counts, moves_pad,
):
    step, part = pl.program_id(0), pl.program_id(1)
    replica = lax.axis_index("rep")
    kin, kout = left_acc.shape[1], right_acc.shape[1]
    slots, width = sums.shape
    doc_slots = moves_ref.shape[1]
    contract = (((1,), (1,)), ((), ()))
    left_part = lax.dot_general(acts_ref[...], in_ref[...], contract, preferred_element_type=F32)
    right_part = lax.dot_general(grads_ref[...], out_ref[...], contract, preferred_element_type=F32)

    @pl.when(part == 0)
    def _():
        left_acc[...] = left_part
        right_acc[...] = right_part

    @pl.when(part > 0)
    def _():
        left_acc[...] += left_part
        right_acc[...] += right_part

    @pl.when((step == 0) & (part == 0))
    def _():
        sums[...] = jnp.zeros_like(sums)
        counts[...] = jnp.zeros_like(counts)
        moves_pad[...] = jnp.full_like(moves_pad, -1)
        moves_pad[:, :doc_slots] = moves_ref[...]

    @pl.when(part == steps_k - 1)
    def _():
        left = left_acc[...].astype(BF16)
        right = right_acc[...].astype(BF16)
        lane, sub = iota((kin, width), 1), iota((kin, width), 0)
        spread = onehot(lane // kout == sub)
        lane, sub = iota((kout, width), 1), iota((kout, width), 0)
        repeat = onehot(lane % kout == sub)
        hi, lo = split(dot(left, spread) * dot(right, repeat))
        here = segs_ref[:, pl.ds(pl.multiple_of(step * TOK, TOK), TOK)]
        slot = iota((slots, TOK), 0)
        slot = jnp.where(slot == doc_slots, -1, slot)
        member = onehot(slot == here, F32)
        member_low = member.astype(BF16)
        sums[...] += dot(member_low, hi) + dot(member_low, lo)
        counts[...] += jnp.broadcast_to(jnp.sum(member, axis=1, keepdims=True), counts.shape)

    @pl.when((step == pl.num_programs(0) - 1) & (part == steps_k - 1))
    def _():
        total, count = sums[...], counts[...]
        moves = moves_pad[...]
        last = jnp.max(segs_ref[...], axis=1, keepdims=True)
        lanes = moves.shape[1]
        scale = 1.0 / jnp.sqrt(jnp.maximum(count, 1.0))
        scale = jnp.concatenate([scale] * (width // scale.shape[1]), axis=1)
        local = (total * scale).astype(BF16)
        local = jnp.concatenate([local, jnp.zeros((lanes - slots, width), BF16)], axis=0)
        row, slot = iota((3 * BAL, lanes), 0), iota((3 * BAL, lanes), 1)
        offset = jnp.where(row < BAL, 0, jnp.where(row < 2 * BAL, -1, 1))
        target = (replica + offset) * BAL + row % BAL
        chosen = (moves == target) & (moves >= 0) & (slot != last)
        arr_ref[...] = dot(onehot(chosen), local).astype(BF16)
        is_last = iota((slots, width), 0) == last
        last_sum = jnp.sum(jnp.where(is_last, total, 0.0), axis=0, keepdims=True)
        is_last = iota(counts.shape, 0) == last
        last_count = jnp.sum(jnp.where(is_last, count, 0.0), axis=0, keepdims=True)
        goes_to = jnp.sum(jnp.where(iota(moves.shape, 1) == last, moves, 0), axis=1, keepdims=True)
        row = iota((8, width), 0)
        wide = [last_sum, total[doc_slots : doc_slots + 1]]
        wide += [jnp.broadcast_to(v[:, :1], (1, width)) for v in (last_count, count[doc_slots : doc_slots + 1])]
        wide += [jnp.broadcast_to(goes_to.astype(F32), (1, width))]
        aux = jnp.zeros((8, width), F32)
        for i, v in enumerate(wide):
            aux = jnp.where(row == i, v, aux)
        aux_ref[...] = aux


def front(acts, grads, in_proj, out_proj, segs, moves, steps_k=2):
    tokens, depth = acts.shape
    kin, kout = in_proj.shape[0], out_proj.shape[0]
    width = kin * kout
    cut = depth // steps_k
    slots = -(-(moves.shape[1] + 1) // 16) * 16
    whole = lambda i, k: (0, 0)
    return pl.pallas_call(
        functools.partial(front_kernel, steps_k),
        grid=(tokens // TOK, steps_k),
        in_specs=[
            pl.BlockSpec((TOK, cut), lambda i, k: (i, k)),
            pl.BlockSpec((TOK, cut), lambda i, k: (i, k)),
            pl.BlockSpec((kin, cut), lambda i, k: (0, k)),
            pl.BlockSpec((kout, cut), lambda i, k: (0, k)),
            pl.BlockSpec(segs.shape, whole),
            pl.BlockSpec(moves.shape, whole),
        ],
        out_specs=(pl.BlockSpec((3 * BAL, width), whole), pl.BlockSpec((8, width), whole)),
        out_shape=(
            jax.ShapeDtypeStruct((3 * BAL, width), BF16),
            jax.ShapeDtypeStruct((8, width), F32),
        ),
        scratch_shapes=[
            pltpu.VMEM((TOK, kin), F32),
            pltpu.VMEM((TOK, kout), F32),
            pltpu.VMEM((slots, width), F32),
            pltpu.VMEM((slots, 128), F32),
            pltpu.VMEM((1, 128), jnp.int32),
        ],
        compiler_params=pltpu.CompilerParams(vmem_limit_bytes=40 * 2**20),
    )(acts, grads, in_proj, out_proj, segs, moves)


def gather_kernel(side, cores, arr_ref, aux_ref, all_ref, from_right, from_left, aux_in, ex_send, ex_recv, send, recv):
    n_rep = side * side * cores
    width = all_ref.shape[1]
    me = lax.axis_index("rep")
    core = me % cores
    spot_z = (me // cores) % side
    spot_x = me // (cores * side)

    def rep_at(dx, dz, c):
        x, z = (spot_x + dx + side) % side, (spot_z + dz + side) % side
        return (x * side + z) * cores + c

    right, left, left2 = (me + 1) % n_rep, (me + n_rep - 1) % n_rep, (me + n_rep - 2) % n_rep
    right2 = (me + 2) % n_rep
    sibling = rep_at(0, 0, 1 - core)
    around = [rep_at(1, 0, core), rep_at(-1, 0, core), rep_at(0, 1, core), rep_at(0, -1, core)]
    barrier = pltpu.get_barrier_semaphore()
    senders = [right, left, right2, sibling] + around
    for device in senders:
        pl.semaphore_signal(barrier, inc=1, device_id={"rep": device}, device_id_type=pl.DeviceIdType.MESH)
    pl.semaphore_wait(barrier, len(senders))

    def copy(src, dst, s, r, device):
        return pltpu.make_async_remote_copy(
            src_ref=src, dst_ref=dst, send_sem=s, recv_sem=r,
            device_id={"rep": device}, device_id_type=pl.DeviceIdType.MESH,
        )

    first = [
        copy(aux_ref, aux_in.at[0], ex_send.at[0], ex_recv.at[0], left),
        copy(aux_ref, aux_in.at[1], ex_send.at[1], ex_recv.at[1], right),
        copy(aux_ref, aux_in.at[2], ex_send.at[2], ex_recv.at[2], left2),
        copy(arr_ref.at[pl.ds(BAL, BAL)], from_right, ex_send.at[3], ex_recv.at[3], left),
        copy(arr_ref.at[pl.ds(2 * BAL, BAL)], from_left, ex_send.at[4], ex_recv.at[4], right),
    ]
    for c in first:
        c.start()
    for c in first:
        c.wait_recv()

    mine = arr_ref[pl.ds(0, BAL), :].astype(F32) + from_right[...].astype(F32) + from_left[...].astype(F32)
    own = aux_ref[...]
    after, before, after2 = aux_in[0], aux_in[1], aux_in[2]
    row = iota((BAL, width), 0).astype(F32)
    base = (me * BAL).astype(F32)
    for a, b in ((before, own), (own, after), (after, after2)):
        length = jnp.maximum(a[2:3] + b[3:4], 1.0)
        feature = (a[0:1] + b[1:2]) * (1.0 / jnp.sqrt(length))
        mine = jnp.where(row == a[4:5] - base, feature, mine)
    all_ref[pl.ds(pl.multiple_of(me * BAL, BAL), BAL), :] = mine.astype(BF16)

    half, quarter = width // 2, width // 4
    sent = []

    def piece(dx, dz, c, col, cols):
        start = pl.multiple_of(rep_at(dx, dz, c) * BAL, BAL)
        return all_ref.at[pl.ds(start, BAL), pl.ds(col, cols)]

    def start(index, dx, dz, col, cols, device):
        ref = piece(dx, dz, core, col, cols)
        c = copy(ref, ref, send.at[index], recv.at[index], device)
        c.start()
        sent.append(c)

    def arrived(index, dx, dz, c, col, cols):
        ref = piece(dx, dz, c, col, cols)
        copy(ref, ref, send.at[index], recv.at[index], sibling).wait_recv()

    def place(kind, du, dv):
        return (du, dv) if kind == 0 else (dv, du)

    def to(kind, du, dv):
        return rep_at(*place(kind, du, dv), core)

    order = (0, -1, 1, 2)
    per_kind = 36

    def first_hop(kind):
        col, n = kind * half, kind * per_kind
        start(n + 0, 0, 0, col, half, to(kind, 1, 0))
        start(n + 1, 0, 0, col, half, to(kind, -1, 0))

    def across(kind, d):
        col, n = kind * half, kind * per_kind + 4 + 4 * order.index(d)
        at = place(kind, d, 0)
        start(n + 0, *at, col, half, to(kind, 0, 1))
        start(n + 1, *at, col, half, to(kind, 0, -1))

    def share(kind, du, dv):
        n = kind * per_kind + 20 + 4 * order.index(du) + order.index(dv)
        start(n, *place(kind, du, dv), kind * half, half, sibling)

    def relay(kind, d):
        col, n = kind * half, kind * per_kind + 4 + 4 * order.index(d)
        at = place(kind, d, -1)
        arrived(n + 0, *at, core, col, half)
        start(n + 2, *at, col, quarter, to(kind, 0, 1))
        share(kind, d, -1)
        at = place(kind, d, 1)
        arrived(n + 1, *at, core, col, half)
        start(n + 3, *at, col + quarter, quarter, to(kind, 0, -1))
        share(kind, d, 1)

    def finish(kind, d):
        col, n = kind * half, kind * per_kind + 4 + 4 * order.index(d)
        at = place(kind, d, 2)
        arrived(n + 2, *at, core, col, quarter)
        arrived(n + 3, *at, core, col + quarter, quarter)
        share(kind, d, 2)

    for kind in (0, 1):
        first_hop(kind)
    for kind in (0, 1):
        across(kind, 0)
    for kind in (0, 1):
        share(kind, 0, 0)
    for sign, q in ((-1, 0), (1, 1)):
        for kind in (0, 1):
            col, n = kind * half, kind * per_kind
            at = place(kind, sign, 0)
            arrived(n + q, *at, core, col, half)
            start(n + 2 + q, *at, col + q * quarter, quarter, to(kind, -sign, 0))
            across(kind, sign)
            share(kind, sign, 0)
    for kind in (0, 1):
        relay(kind, 0)
    for kind in (0, 1):
        col, n = kind * half, kind * per_kind
        at = place(kind, 2, 0)
        arrived(n + 2, *at, core, col, quarter)
        arrived(n + 3, *at, core, col + quarter, quarter)
        across(kind, 2)
        share(kind, 2, 0)
    for d in (-1, 1, 2):
        for kind in (0, 1):
            relay(kind, d)
    for d in order:
        for kind in (0, 1):
            finish(kind, d)
    for kind in (0, 1):
        for i, du in enumerate(order):
            for j, dv in enumerate(order):
                n = kind * per_kind + 20 + 4 * i + j
                arrived(n, *place(kind, du, dv), 1 - core, kind * half, half)
    for c in first + sent:
        c.wait_send()


def gather(arr, aux, n_rep):
    width = arr.shape[1]
    cores = 2
    side = round((n_rep // cores) ** 0.5)
    return pl.pallas_call(
        functools.partial(gather_kernel, side, cores),
        out_shape=jax.ShapeDtypeStruct((BAL * n_rep, width), BF16),
        in_specs=[VMEM, VMEM],
        out_specs=VMEM,
        scratch_shapes=[
            pltpu.VMEM((BAL, width), BF16),
            pltpu.VMEM((BAL, width), BF16),
            pltpu.VMEM((3, 8, width), F32),
            pltpu.SemaphoreType.DMA((5,)),
            pltpu.SemaphoreType.DMA((5,)),
            pltpu.SemaphoreType.DMA((72,)),
            pltpu.SemaphoreType.DMA((72,)),
        ],
        compiler_params=pltpu.CompilerParams(
            collective_id=0, has_side_effects=True, vmem_limit_bytes=16 * 2**20
        ),
    )(arr, aux)


def pivot_rows(D, V):
    size, width = V.shape
    tiles, strips = size // 8, width // 128
    row = iota((8, 128), 0)
    cols = [
        [jnp.broadcast_to(D[8 * i : 8 * i + 8, j : j + 1], (8, 128)) if i >= j // 8 else None for i in range(tiles)]
        for j in range(size)
    ]
    rows = [[V[8 * i : 8 * i + 8, 128 * c : 128 * c + 128] for c in range(strips)] for i in range(tiles)]
    pivots = [jnp.ones((8, 128), F32) for _ in range(tiles)]
    for j in range(size):
        tile, sub = divmod(j, 8)
        column = cols[j]
        pivot = jnp.broadcast_to(column[tile][sub : sub + 1], (8, 128))
        inverse = 1.0 / pivot
        pivots[tile] = jnp.where(row == sub, pivot, pivots[tile])
        factor = [column[i] * inverse if i >= tile else None for i in range(tiles)]
        for j2 in range(j + 1, size):
            other = jnp.broadcast_to(column[j2 // 8][j2 % 8 : j2 % 8 + 1], (8, 128))
            for i in range(j2 // 8, tiles):
                cols[j2][i] = cols[j2][i] - factor[i] * other
        for c in range(strips):
            source = jnp.broadcast_to(rows[tile][c][sub : sub + 1], (8, 128))
            for i in range(tile, tiles):
                weight = jnp.where(row > sub, factor[i], 0.0) if i == tile else factor[i]
                rows[i][c] = rows[i][c] - weight * source
    out = []
    for i in range(tiles):
        scale = lax.rsqrt(pivots[i])
        out.append(jnp.concatenate([rows[i][c] * scale for c in range(strips)], axis=1))
    return jnp.concatenate(out, axis=0)


def factor_block(A):
    same = iota((BLOCK, BLOCK), 0) == iota((BLOCK, BLOCK), 1)
    V = jnp.concatenate([A, onehot(same, F32)], axis=1)
    done = []
    for at in range(0, BLOCK, GROUP):
        rows = pivot_rows(V[:GROUP, at : at + GROUP], V[:GROUP])
        done.append(rows)
        if at + GROUP < BLOCK:
            hi, lo = split(rows)
            here = jnp.concatenate([hi, hi, lo], axis=0)[:, at + GROUP : BLOCK]
            V = V[GROUP:] - dot_t(here, jnp.concatenate([hi, lo, hi], axis=0))
    both = jnp.concatenate(done, axis=0)
    return both[:, :BLOCK], both[:, BLOCK:]


def factor_kernel(all_ref, fac_ref, mine_ref, quad_ref, high, low):
    docs, n = all_ref.shape
    width = n + 128
    replica = lax.axis_index("rep")
    mine = all_ref[pl.ds(pl.multiple_of(replica * BAL, BAL), BAL), :]
    mine_ref[...] = mine
    ri, ci = iota((BLOCK, BLOCK), 0), iota((BLOCK, BLOCK), 1)
    quad = jnp.zeros((1, 128), F32)
    for a in range(0, n, BLOCK):
        b = a + BLOCK
        hessian = dot_t(all_ref[:, a:b], all_ref[:, a:n]) * (1.0 / docs)
        extra = mine[:, a:b].astype(F32).T
        extra = jnp.concatenate([extra, jnp.zeros((BLOCK, 128 - BAL), F32)], axis=1)
        panel = jnp.concatenate([hessian, extra], axis=1)
        if a > 0:
            lh, ll = high[:a, a:b], low[:a, a:b]
            gh, gl = high[:a, a:width], low[:a, a:width]
            panel = panel - (dot_t(lh, gh) + dot_t(lh, gl) + dot_t(ll, gh))
        upper, inverse = factor_block(panel[:, :BLOCK] + jnp.where(ri == ci, DAMPING, 0.0))
        fac_ref[a:b, a:b] = jnp.where(ci >= ri, upper, 0.0)
        th, tl = split(inverse)
        sh, sl = split(panel[:, BLOCK:])
        solved = dot(th, sh) + dot(th, sl) + dot(tl, sh)
        if b < n:
            fac_ref[a:b, b:n] = solved[:, : n - b]
            hi, lo = split(solved)
            high[a:b, b:width] = hi
            low[a:b, b:width] = lo
        if a > 0:
            fac_ref[a:b, :a] = jnp.zeros((BLOCK, a), F32)
        tail = solved[:, n - b :]
        quad = quad + jnp.sum(tail * tail, axis=0, keepdims=True)
    quad_ref[...] = jnp.broadcast_to(quad * (1.0 / n), quad_ref.shape)


def factor(everyone):
    docs, n = everyone.shape
    return pl.pallas_call(
        factor_kernel,
        out_shape=(
            jax.ShapeDtypeStruct((n, n), F32),
            jax.ShapeDtypeStruct((BAL, n), BF16),
            jax.ShapeDtypeStruct((8, 128), F32),
        ),
        in_specs=[VMEM],
        out_specs=(VMEM, VMEM, VMEM),
        scratch_shapes=[pltpu.VMEM((n, n + 128), BF16), pltpu.VMEM((n, n + 128), BF16)],
        compiler_params=pltpu.CompilerParams(vmem_limit_bytes=40 * 2**20),
    )(everyone)


def layer_sum_kernel(layers, quad_ref, out_ref, inbox, send, recv):
    me = lax.axis_index("layer")
    barrier = pltpu.get_barrier_semaphore()
    for step in range(1, layers):
        device = (me + step) % layers
        pl.semaphore_signal(barrier, inc=1, device_id={"layer": device}, device_id_type=pl.DeviceIdType.MESH)
    pl.semaphore_wait(barrier, layers - 1)
    copies = []
    for step in range(1, layers):
        copies.append(
            pltpu.make_async_remote_copy(
                src_ref=quad_ref, dst_ref=inbox.at[step - 1], send_sem=send.at[step - 1],
                recv_sem=recv.at[step - 1], device_id={"layer": (me + step) % layers},
                device_id_type=pl.DeviceIdType.MESH,
            )
        )
        copies[-1].start()
    total = quad_ref[...]
    for step, c in enumerate(copies):
        c.wait_recv()
        total = total + inbox[step]
    out_ref[...] = total[:1, :BAL]
    for c in copies:
        c.wait_send()


def layer_sum(quad, layers):
    return pl.pallas_call(
        functools.partial(layer_sum_kernel, layers),
        out_shape=jax.ShapeDtypeStruct((1, BAL), F32),
        in_specs=[VMEM],
        out_specs=VMEM,
        scratch_shapes=[
            pltpu.VMEM((layers - 1,) + quad.shape, F32),
            pltpu.SemaphoreType.DMA((layers - 1,)),
            pltpu.SemaphoreType.DMA((layers - 1,)),
        ],
        compiler_params=pltpu.CompilerParams(collective_id=1, has_side_effects=True),
    )(quad)


def on_device(n_rep, layers, activations, output_grads, in_projection, out_projection, segment_ids, move_list):
    arranged, aux = front(
        activations[0], output_grads[0], in_projection[0], out_projection[0],
        segment_ids[None], move_list[None],
    )
    everyone = gather(arranged, aux, n_rep)
    upper, mine, quad = factor(everyone)
    influence = layer_sum(quad, layers)
    return (upper[None], mine[None], influence[0])


def solution(mesh):
    placed = (
        PartitionSpec("layer", "rep", None),
        PartitionSpec("layer", "rep", None),
        PartitionSpec("layer", None, None),
        PartitionSpec("layer", None, None),
        PartitionSpec("rep"),
        PartitionSpec("rep"),
    )
    return jax.shard_map(
        functools.partial(on_device, mesh.shape["rep"], mesh.shape["layer"]),
        mesh=mesh,
        in_specs=placed,
        out_specs=(PartitionSpec("layer", None, None), PartitionSpec("layer", "rep", None), PartitionSpec("rep")),
        check_vma=False,
    )
```

time: 530 us -> 90.6 us (0.17); the launches traced: 521 us -> 90.2 us
  other arithmetic: 267 us -> 0 us
  waiting for transfers between devices: 122 us -> 0 us
  Pallas kernels: 0 us -> 81 us
  matrix products: 52.1 us -> 0 us
  local copies, waits for them, and re-layouts: 39.6 us -> 8.56 us
  between operations: 20.2 us -> 0.67 us
  starting transfers between devices: 10.9 us -> 0 us
  blocking collectives: 8.97 us -> 0 us
    another operation x33 -> x0, other arithmetic: 253 us -> none  [the longest x30 167 us: on_device(): lower = jnp.linalg.cholesky(hessian)]
    psum x1 -> x0, waiting for transfers between devices: 118 us -> none  [on_device(): gram = lax.psum(local_gram, 'rep')]
    pallas_call x0 -> x4, Pallas kernels: none -> 81 us  [the longest x1 33.6 us: factor(): pl.pallas_call(factor_kernel, out_shape=(jax.ShapeDtypeStruct((n, n), F32...]
    another operation x29 -> x0, matrix products: 36 us -> none  [the longest x14 26.2 us: on_device(): lower = jnp.linalg.cholesky(hessian)]
    another operation x66 -> x0, local copies, waits for them, and re-layouts: 29.2 us -> none
    dot_general x6 -> x0, matrix products: 16.1 us -> none  [the longest x1 6.67 us: on_device(): lax.dot_general(masked, right, (((2,), (1,)), ((), ())), preferred_elemen...]
    ppermute x4 -> x0, starting transfers between devices: 10.8 us -> none  [shifted(): return lax.ppermute(block, axis, route)]
    psum x1 -> x0, blocking collectives: 8.97 us -> none  [on_device(): influence = lax.psum(quad, 'layer')]
  transfers between devices with their start and end apart: 5 -> 0, of which waited for: 2 -> 0; matrix products, arithmetic and copies ran while one was open for 3% -> 0% of each run, Pallas kernels for 0% -> 0%
where the time goes in v2:
time: 90.6 us; the launch traced here: 90.2 us
  Pallas kernels  81 us (89%)
  local copies, waits for them, and re-layouts  8.56 us (9%)
    pallas_call x1, Pallas kernels, factor(): pl.pallas_call(factor_kernel, out_shape=(jax.ShapeDtypeStruct((n, n), F32...  33.6 us
    pallas_call x1, Pallas kernels, gather(): pl.pallas_call(functools.partial(gather_kernel, side, cores), out_shape=j...  30 us
    pallas_call x1, Pallas kernels, front(): pl.pallas_call(functools.partial(front_kernel, steps_k), grid=(tokens //...  11.2 us
    unnamed x13, local copies, waits for them, and re-layouts  8.56 us
    pallas_call x1, Pallas kernels, layer_sum(): pl.pallas_call(functools.partial(layer_sum_kernel, layers), out_shape=jax...  6.26 us

profile of v2, /device:TPU:1, one launch (start us, length us, event | category | flops | bytes accessed | tf_op | source)
XLA Modules:
  0.0 90.2 jit_solution(1051519118977408872)
XLA Ops:
  0.6 0.0 copy-start
  0.6 3.4 %copy-done = bf16[1,512,8192]{2,1,0:T(8,128)(2,1)S(1)} copy-done((bf16[1,512,8192]{2,1,0:T(8,128)(2,1)S(1)}, bf16[1,512,8192]{2,1,0:T(8,128)(2,1)}, u32[]{:S(2)}) %copy-start) | copy-done | bytes 8388632
  4.0 0.0 copy-start.1
  4.0 1.0 %copy-done.1 = bf16[1,32,8192]{2,1,0:T(8,128)(2,1)S(1)} copy-done((bf16[1,32,8192]{2,1,0:T(8,128)(2,1)S(1)}, bf16[1,32,8192]{2,1,0:T(8,128)(2,1)}, u32[]{:S(2)}) %copy-start.1) | copy-done | bytes 524312
  5.1 0.0 copy-start.2
  5.1 1.0 %copy-done.2 = bf16[1,32,8192]{2,1,0:T(8,128)(2,1)S(1)} copy-done((bf16[1,32,8192]{2,1,0:T(8,128)(2,1)S(1)}, bf16[1,32,8192]{2,1,0:T(8,128)(2,1)}, u32[]{:S(2)}) %copy-start.2) | copy-done | bytes 524312
  6.1 0.0 copy-start.4
  6.1 0.7 copy-done.4
  6.8 0.0 copy-start.5
  6.8 0.7 copy-done.5
  7.4 11.2 %shard_map.85 = (bf16[96,1024]{1,0:T(8,128)(2,1)S(1)}, f32[8,1024]{1,0:T(8,128)S(1)}) custom-call(bf16[512,8192]{1,0:T(8,128)(2,1)S(1)} %bitcast.9, bf16[512,8192]{1,0:T(8,128)(2,1)} %bitcast.14, bf16[32,8192]{1,0:T(8,128)(2,1)S(1)} %bitcast.10, bf16[32,8192]{1,0:T(8,128)(2,1)S(1)} %bitcast.11, s32[1,512]{1,0:T(1,128)S(1)} %bitcast.12, s32[1,62]{1,0:T(1,128)S(1)} %bitcast.13), custom_call_target="tpu_custom_call" | custom-call | tf_op jit(solution)/shard_map/pallas_call | solution.py:126
  18.6 30.0 %shard_map.86.all_ref = bf16[1024,1024]{1,0:T(8,128)(2,1)S(1)} custom-call(bf16[96,1024]{1,0:T(8,128)(2,1)S(1)} %get-tuple-element.8.arr_ref, f32[8,1024]{1,0:T(8,128)S(1)} %get-tuple-element.9.aux_ref), custom_call_target="tpu_custom_call" | custom-call | tf_op jit(solution)/shard_map/pallas_call | solution.py:305
  48.6 33.6 %shard_map.87 = (f32[1024,1024]{1,0:T(8,128)}, bf16[32,1024]{1,0:T(8,128)(2,1)}, f32[8,128]{1,0:T(8,128)S(1)}) custom-call(bf16[1024,1024]{1,0:T(8,128)(2,1)S(1)} %shard_map.86.all_ref), custom_call_target="tpu_custom_call" | custom-call | tf_op jit(solution)/shard_map/pallas_call | solution.py:410
  82.1 0.0 copy-start.3
  82.1 0.6 copy-done.3
  82.7 6.3 %shard_map.88 = f32[1,32]{1,0:T(1,128)} custom-call(f32[8,128]{1,0:T(8,128)} %copy-done.3), custom_call_target="tpu_custom_call" | custom-call | tf_op jit(solution)/shard_map/pallas_call | solution.py:451
  89.0 1.2 %copy.10 = f32[32]{0:T(128)} copy(f32[32]{0:T(128)} %bitcast.15) | data formatting | bytes 256
Async XLA Ops:
  0.6 3.4 %copy-start = (bf16[1,512,8192]{2,1,0:T(8,128)(2,1)S(1)}, bf16[1,512,8192]{2,1,0:T(8,128)(2,1)}, u32[]{:S(2)}) copy-start(bf16[1,512,8192]{2,1,0:T(8,128)(2,1)} %param.6) | copy-start | bytes 25165828
  4.0 1.0 %copy-start.1 = (bf16[1,32,8192]{2,1,0:T(8,128)(2,1)S(1)}, bf16[1,32,8192]{2,1,0:T(8,128)(2,1)}, u32[]{:S(2)}) copy-start(bf16[1,32,8192]{2,1,0:T(8,128)(2,1)} %param.8) | copy-start | bytes 1572868
  5.1 1.0 %copy-start.2 = (bf16[1,32,8192]{2,1,0:T(8,128)(2,1)S(1)}, bf16[1,32,8192]{2,1,0:T(8,128)(2,1)}, u32[]{:S(2)}) copy-start(bf16[1,32,8192]{2,1,0:T(8,128)(2,1)} %param.9) | copy-start | bytes 1572868
  6.1 0.7 copy-start.4
  6.8 0.7 copy-start.5
  82.1 0.6 copy-start.3

commit v3 on v2

--- a/solution.py
+++ b/solution.py
@@ -11,7 +11,6 @@
 BLOCK = 128
 GROUP = 32
 DAMPING = 0.05
-TOK = 128
 F32 = jnp.float32
 BF16 = jnp.bfloat16
 VMEM = pl.BlockSpec(memory_space=pltpu.VMEM)
@@ -38,113 +37,146 @@
 def onehot(mask, dtype=BF16):
     return jnp.where(mask, 1.0, 0.0).astype(dtype)
 
+CHUNKS = (64, 128, 128, 128, 64)
+AHEAD = 2
+
+
+def project(block, proj):
+    contract = (((1,), (1,)), ((), ()))
+    return lax.dot_general(block, proj, contract, preferred_element_type=F32).astype(BF16)
+
+
+def expand(x, pattern):
+    return dot(x, pattern)
+
 
 def front_kernel(
-    steps_k, acts_ref, grads_ref, in_ref, out_ref, segs_ref, moves_ref,
-    arr_ref, aux_ref, left_acc, right_acc, sums, counts, moves_pad,
+    acts_hbm, grads_hbm, in_hbm, out_hbm, segs_hbm, moves_hbm, arr_ref, aux_ref,
+    acts, grads, in_proj, out_proj, segs, moves_in, sums, counts, moves_pad, sem, small_sem,
 ):
-    step, part = pl.program_id(0), pl.program_id(1)
     replica = lax.axis_index("rep")
-    kin, kout = left_acc.shape[1], right_acc.shape[1]
+    kin, kout = in_proj.shape[0], out_proj.shape[0]
     slots, width = sums.shape
-    doc_slots = moves_ref.shape[1]
-    contract = (((1,), (1,)), ((), ()))
-    left_part = lax.dot_general(acts_ref[...], in_ref[...], contract, preferred_element_type=F32)
-    right_part = lax.dot_general(grads_ref[...], out_ref[...], contract, preferred_element_type=F32)
-
-    @pl.when(part == 0)
-    def _():
-        left_acc[...] = left_part
-        right_acc[...] = right_part
-
-    @pl.when(part > 0)
-    def _():
-        left_acc[...] += left_part
-        right_acc[...] += right_part
-
-    @pl.when((step == 0) & (part == 0))
-    def _():
-        sums[...] = jnp.zeros_like(sums)
-        counts[...] = jnp.zeros_like(counts)
-        moves_pad[...] = jnp.full_like(moves_pad, -1)
-        moves_pad[:, :doc_slots] = moves_ref[...]
-
-    @pl.when(part == steps_k - 1)
-    def _():
-        left = left_acc[...].astype(BF16)
-        right = right_acc[...].astype(BF16)
-        lane, sub = iota((kin, width), 1), iota((kin, width), 0)
-        spread = onehot(lane // kout == sub)
-        lane, sub = iota((kout, width), 1), iota((kout, width), 0)
-        repeat = onehot(lane % kout == sub)
-        hi, lo = split(dot(left, spread) * dot(right, repeat))
-        here = segs_ref[:, pl.ds(pl.multiple_of(step * TOK, TOK), TOK)]
-        slot = iota((slots, TOK), 0)
+    doc_slots = moves_in.shape[1]
+    small = [
+        pltpu.make_async_copy(a, b, small_sem.at[i])
+        for i, (a, b) in enumerate(
+            ((in_hbm, in_proj), (out_hbm, out_proj), (segs_hbm, segs), (moves_hbm, moves_in))
+        )
+    ]
+    large = []
+    ends = [sum(CHUNKS[: c + 1]) for c in range(len(CHUNKS))]
+    for c, size in enumerate(CHUNKS):
+        rows = pl.ds(ends[c] - size, size)
+        large.append(
+            (
+                pltpu.make_async_copy(acts_hbm.at[rows], acts.at[rows], sem.at[0, c]),
+                pltpu.make_async_copy(grads_hbm.at[rows], grads.at[rows], sem.at[1, c]),
+            )
+        )
+    small[0].start()
+    small[1].start()
+    for pair in large[:AHEAD]:
+        pair[0].start()
+        pair[1].start()
+    small[2].start()
+    small[3].start()
+    lane, sub = iota((kin, width), 1), iota((kin, width), 0)
+    spread = onehot(lane // kout == sub)
+    lane, sub = iota((kout, width), 1), iota((kout, width), 0)
+    repeat = onehot(lane % kout == sub)
+    moves_pad[...] = jnp.full_like(moves_pad, -1)
+    def gather_documents(c, left, right):
+        hi, lo = split(expand(left, spread) * expand(right, repeat))
+        size = CHUNKS[c]
+        here = segs[:, ends[c] - size : ends[c]]
+        slot = iota((slots, size), 0)
         slot = jnp.where(slot == doc_slots, -1, slot)
         member = onehot(slot == here, F32)
         member_low = member.astype(BF16)
-        sums[...] += dot(member_low, hi) + dot(member_low, lo)
-        counts[...] += jnp.broadcast_to(jnp.sum(member, axis=1, keepdims=True), counts.shape)
-
-    @pl.when((step == pl.num_programs(0) - 1) & (part == steps_k - 1))
-    def _():
-        total, count = sums[...], counts[...]
-        moves = moves_pad[...]
-        last = jnp.max(segs_ref[...], axis=1, keepdims=True)
-        lanes = moves.shape[1]
-        scale = 1.0 / jnp.sqrt(jnp.maximum(count, 1.0))
-        scale = jnp.concatenate([scale] * (width // scale.shape[1]), axis=1)
-        local = (total * scale).astype(BF16)
-        local = jnp.concatenate([local, jnp.zeros((lanes - slots, width), BF16)], axis=0)
-        row, slot = iota((3 * BAL, lanes), 0), iota((3 * BAL, lanes), 1)
-        offset = jnp.where(row < BAL, 0, jnp.where(row < 2 * BAL, -1, 1))
-        target = (replica + offset) * BAL + row % BAL
-        chosen = (moves == target) & (moves >= 0) & (slot != last)
-        arr_ref[...] = dot(onehot(chosen), local).astype(BF16)
-        is_last = iota((slots, width), 0) == last
-        last_sum = jnp.sum(jnp.where(is_last, total, 0.0), axis=0, keepdims=True)
-        is_last = iota(counts.shape, 0) == last
-        last_count = jnp.sum(jnp.where(is_last, count, 0.0), axis=0, keepdims=True)
-        goes_to = jnp.sum(jnp.where(iota(moves.shape, 1) == last, moves, 0), axis=1, keepdims=True)
-        row = iota((8, width), 0)
-        wide = [last_sum, total[doc_slots : doc_slots + 1]]
-        wide += [jnp.broadcast_to(v[:, :1], (1, width)) for v in (last_count, count[doc_slots : doc_slots + 1])]
-        wide += [jnp.broadcast_to(goes_to.astype(F32), (1, width))]
-        aux = jnp.zeros((8, width), F32)
-        for i, v in enumerate(wide):
-            aux = jnp.where(row == i, v, aux)
-        aux_ref[...] = aux
-
-
-def front(acts, grads, in_proj, out_proj, segs, moves, steps_k=2):
+        part = dot(member_low, hi) + dot(member_low, lo)
+        number = jnp.broadcast_to(jnp.sum(member, axis=1, keepdims=True), counts.shape)
+        if c == 0:
+            sums[...] = part
+            counts[...] = number
+        else:
+            sums[...] += part
+            counts[...] += number
+
+    held = None
+    for copy in small:
+        copy.wait()
+    for c, size in enumerate(CHUNKS):
+        rows = pl.ds(ends[c] - size, size)
+        for copy in large[c]:
+            copy.wait()
+        if c + AHEAD < len(CHUNKS):
+            for copy in large[c + AHEAD]:
+                copy.start()
+        left = project(acts[rows, :], in_proj[...])
+        right = project(grads[rows, :], out_proj[...])
+        if c > 0:
+            gather_documents(c - 1, *held)
+        held = left, right
+    gather_documents(len(CHUNKS) - 1, *held)
+    moves_pad[:, :doc_slots] = moves_in[...]
+    total, count = sums[...], counts[...]
+    moves = moves_pad[...]
+    last = jnp.max(segs[...], axis=1, keepdims=True)
+    lanes = moves.shape[1]
+    scale = 1.0 / jnp.sqrt(jnp.maximum(count, 1.0))
+    scale = jnp.concatenate([scale] * (width // scale.shape[1]), axis=1)
+    local = (total * scale).astype(BF16)
+    local = jnp.concatenate([local, jnp.zeros((lanes - slots, width), BF16)], axis=0)
+    row, slot = iota((3 * BAL, lanes), 0), iota((3 * BAL, lanes), 1)
+    offset = jnp.where(row < BAL, 0, jnp.where(row < 2 * BAL, -1, 1))
+    target = (replica + offset) * BAL + row % BAL
+    chosen = (moves == target) & (moves >= 0) & (slot != last)
+    arr_ref[...] = dot(onehot(chosen), local).astype(BF16)
+    is_last = iota((slots, width), 0) == last
+    last_sum = jnp.sum(jnp.where(is_last, total, 0.0), axis=0, keepdims=True)
+    is_last = iota(counts.shape, 0) == last
+    last_count = jnp.sum(jnp.where(is_last, count, 0.0), axis=0, keepdims=True)
+    goes_to = jnp.sum(jnp.where(iota(moves.shape, 1) == last, moves, 0), axis=1, keepdims=True)
+    row = iota((8, width), 0)
+    wide = [last_sum, total[doc_slots : doc_slots + 1]]
+    wide += [jnp.broadcast_to(v[:, :1], (1, width)) for v in (last_count, count[doc_slots : doc_slots + 1])]
+    wide += [jnp.broadcast_to(goes_to.astype(F32), (1, width))]
+    aux = jnp.zeros((8, width), F32)
+    for i, v in enumerate(wide):
+        aux = jnp.where(row == i, v, aux)
+    aux_ref[...] = aux
+
+
+def front(acts, grads, in_proj, out_proj, segs, moves):
     tokens, depth = acts.shape
     kin, kout = in_proj.shape[0], out_proj.shape[0]
     width = kin * kout
-    cut = depth // steps_k
     slots = -(-(moves.shape[1] + 1) // 16) * 16
-    whole = lambda i, k: (0, 0)
+    acts, grads, in_proj, out_proj, segs, moves = (
+        pltpu.with_memory_space_constraint(v, pltpu.HBM) for v in (acts, grads, in_proj, out_proj, segs, moves)
+    )
+    held = pl.BlockSpec(memory_space=pltpu.HBM)
     return pl.pallas_call(
-        functools.partial(front_kernel, steps_k),
-        grid=(tokens // TOK, steps_k),
-        in_specs=[
-            pl.BlockSpec((TOK, cut), lambda i, k: (i, k)),
-            pl.BlockSpec((TOK, cut), lambda i, k: (i, k)),
-            pl.BlockSpec((kin, cut), lambda i, k: (0, k)),
-            pl.BlockSpec((kout, cut), lambda i, k: (0, k)),
-            pl.BlockSpec(segs.shape, whole),
-            pl.BlockSpec(moves.shape, whole),
-        ],
-        out_specs=(pl.BlockSpec((3 * BAL, width), whole), pl.BlockSpec((8, width), whole)),
+        front_kernel,
+        in_specs=[held] * 6,
+        out_specs=(VMEM, VMEM),
         out_shape=(
             jax.ShapeDtypeStruct((3 * BAL, width), BF16),
             jax.ShapeDtypeStruct((8, width), F32),
         ),
         scratch_shapes=[
-            pltpu.VMEM((TOK, kin), F32),
-            pltpu.VMEM((TOK, kout), F32),
+            pltpu.VMEM(acts.shape, BF16),
+            pltpu.VMEM(grads.shape, BF16),
+            pltpu.VMEM(in_proj.shape, BF16),
+            pltpu.VMEM(out_proj.shape, BF16),
+            pltpu.VMEM(segs.shape, jnp.int32),
+            pltpu.VMEM(moves.shape, jnp.int32),
             pltpu.VMEM((slots, width), F32),
             pltpu.VMEM((slots, 128), F32),
             pltpu.VMEM((1, 128), jnp.int32),
+            pltpu.SemaphoreType.DMA((2, len(CHUNKS))),
+            pltpu.SemaphoreType.DMA((4,)),
         ],
         compiler_params=pltpu.CompilerParams(vmem_limit_bytes=40 * 2**20),
     )(acts, grads, in_proj, out_proj, segs, moves)
@@ -165,7 +197,7 @@
     right, left, left2 = (me + 1) % n_rep, (me + n_rep - 1) % n_rep, (me + n_rep - 2) % n_rep
     right2 = (me + 2) % n_rep
     sibling = rep_at(0, 0, 1 - core)
-    around = [rep_at(1, 0, core), rep_at(-1, 0, core), rep_at(0, 1, core), rep_at(0, -1, core)]
+    around = [rep_at(d, 0, core) for d in (1, -1, 2)] + [rep_at(0, d, core) for d in (1, -1, 2)]
     barrier = pltpu.get_barrier_semaphore()
     senders = [right, left, right2, sibling] + around
     for device in senders:
@@ -201,7 +233,7 @@
         mine = jnp.where(row == a[4:5] - base, feature, mine)
     all_ref[pl.ds(pl.multiple_of(me * BAL, BAL), BAL), :] = mine.astype(BF16)
 
-    half, quarter = width // 2, width // 4
+    half = width // 2
     sent = []
 
     def piece(dx, dz, c, col, cols):
@@ -224,75 +256,46 @@
     def to(kind, du, dv):
         return rep_at(*place(kind, du, dv), core)
 
-    order = (0, -1, 1, 2)
-    per_kind = 36
-
-    def first_hop(kind):
-        col, n = kind * half, kind * per_kind
-        start(n + 0, 0, 0, col, half, to(kind, 1, 0))
-        start(n + 1, 0, 0, col, half, to(kind, -1, 0))
-
-    def across(kind, d):
-        col, n = kind * half, kind * per_kind + 4 + 4 * order.index(d)
-        at = place(kind, d, 0)
-        start(n + 0, *at, col, half, to(kind, 0, 1))
-        start(n + 1, *at, col, half, to(kind, 0, -1))
+    order = (0, 1, -1, 2)
+    per_kind = 3 + 12 + 16
+
+    def along(kind):
+        for i, d in enumerate(order[1:]):
+            start(kind * per_kind + i, 0, 0, kind * half, half, to(kind, d, 0))
+
+    def across(kind, du):
+        at = place(kind, du, 0)
+        for i, d in enumerate(order[1:]):
+            n = kind * per_kind + 3 + 3 * order.index(du) + i
+            start(n, *at, kind * half, half, to(kind, 0, d))
 
     def share(kind, du, dv):
-        n = kind * per_kind + 20 + 4 * order.index(du) + order.index(dv)
+        n = kind * per_kind + 15 + 4 * order.index(du) + order.index(dv)
         start(n, *place(kind, du, dv), kind * half, half, sibling)
 
-    def relay(kind, d):
-        col, n = kind * half, kind * per_kind + 4 + 4 * order.index(d)
-        at = place(kind, d, -1)
-        arrived(n + 0, *at, core, col, half)
-        start(n + 2, *at, col, quarter, to(kind, 0, 1))
-        share(kind, d, -1)
-        at = place(kind, d, 1)
-        arrived(n + 1, *at, core, col, half)
-        start(n + 3, *at, col + quarter, quarter, to(kind, 0, -1))
-        share(kind, d, 1)
-
-    def finish(kind, d):
-        col, n = kind * half, kind * per_kind + 4 + 4 * order.index(d)
-        at = place(kind, d, 2)
-        arrived(n + 2, *at, core, col, quarter)
-        arrived(n + 3, *at, core, col + quarter, quarter)
-        share(kind, d, 2)
+    def back(d):
+        return d if d == 2 else -d
 
     for kind in (0, 1):
-        first_hop(kind)
+        along(kind)
     for kind in (0, 1):
         across(kind, 0)
-    for kind in (0, 1):
         share(kind, 0, 0)
-    for sign, q in ((-1, 0), (1, 1)):
+    for i, d in enumerate(order[1:]):
         for kind in (0, 1):
-            col, n = kind * half, kind * per_kind
-            at = place(kind, sign, 0)
-            arrived(n + q, *at, core, col, half)
-            start(n + 2 + q, *at, col + q * quarter, quarter, to(kind, -sign, 0))
-            across(kind, sign)
-            share(kind, sign, 0)
-    for kind in (0, 1):
-        relay(kind, 0)
-    for kind in (0, 1):
-        col, n = kind * half, kind * per_kind
-        at = place(kind, 2, 0)
-        arrived(n + 2, *at, core, col, quarter)
-        arrived(n + 3, *at, core, col + quarter, quarter)
-        across(kind, 2)
-        share(kind, 2, 0)
-    for d in (-1, 1, 2):
-        for kind in (0, 1):
-            relay(kind, d)
-    for d in order:
-        for kind in (0, 1):
-            finish(kind, d)
+            arrived(kind * per_kind + i, *place(kind, back(d), 0), core, kind * half, half)
+            across(kind, back(d))
+            share(kind, back(d), 0)
+    for du in (0, -1, 1, 2):
+        for i, d in enumerate(order[1:]):
+            for kind in (0, 1):
+                n = kind * per_kind + 3 + 3 * order.index(du) + i
+                arrived(n, *place(kind, du, back(d)), core, kind * half, half)
+                share(kind, du, back(d))
     for kind in (0, 1):
         for i, du in enumerate(order):
             for j, dv in enumerate(order):
-                n = kind * per_kind + 20 + 4 * i + j
+                n = kind * per_kind + 15 + 4 * i + j
                 arrived(n, *place(kind, du, dv), 1 - core, kind * half, half)
     for c in first + sent:
         c.wait_send()
@@ -313,8 +316,8 @@
             pltpu.VMEM((3, 8, width), F32),
             pltpu.SemaphoreType.DMA((5,)),
             pltpu.SemaphoreType.DMA((5,)),
-            pltpu.SemaphoreType.DMA((72,)),
-            pltpu.SemaphoreType.DMA((72,)),
+            pltpu.SemaphoreType.DMA((62,)),
+            pltpu.SemaphoreType.DMA((62,)),
         ],
         compiler_params=pltpu.CompilerParams(
             collective_id=0, has_side_effects=True, vmem_limit_bytes=16 * 2**20
@@ -458,7 +461,9 @@
             pltpu.SemaphoreType.DMA((layers - 1,)),
             pltpu.SemaphoreType.DMA((layers - 1,)),
         ],
-        compiler_params=pltpu.CompilerParams(collective_id=1, has_side_effects=True),
+        compiler_params=pltpu.CompilerParams(
+            collective_id=1, has_side_effects=True, vmem_limit_bytes=2 * 2**20
+        ),
     )(quad)
 
 

time: 90.6 us -> 75.3 us (0.83)
  local copies, waits for them, and re-layouts: 8.56 us -> 0.51 us
  Pallas kernels: 81 us -> 74.1 us
    unnamed x13 -> x1, local copies, waits for them, and re-layouts: 8.56 us -> 0.51 us
    pallas_call x1, Pallas kernels: 30 us -> 25.5 us  [gather(): pl.pallas_call(functools.partial(gather_kernel, side, cores), out_shape=j...]
    pallas_call x1, Pallas kernels: 11.2 us -> 9.6 us  [front(): pl.pallas_call(front_kernel, in_specs=[held] * 6, out_specs=(VMEM, VMEM),...]
    pallas_call x1, Pallas kernels: 6.26 us -> 5 us  [layer_sum(): pl.pallas_call(functools.partial(layer_sum_kernel, layers), out_shape=jax...]
where the time goes in v3:
time: 75.3 us; the launch traced here: 75.2 us
  Pallas kernels  74.1 us (98%)
    pallas_call x1, Pallas kernels, factor(): pl.pallas_call(factor_kernel, out_shape=(jax.ShapeDtypeStruct((n, n), F32...  34 us
    pallas_call x1, Pallas kernels, gather(): pl.pallas_call(functools.partial(gather_kernel, side, cores), out_shape=j...  25.5 us
    pallas_call x1, Pallas kernels, front(): pl.pallas_call(front_kernel, in_specs=[held] * 6, out_specs=(VMEM, VMEM),...  9.6 us
    pallas_call x1, Pallas kernels, layer_sum(): pl.pallas_call(functools.partial(layer_sum_kernel, layers), out_shape=jax...  5 us

profile of v3, /device:TPU:1, one launch (start us, length us, event | category | flops | bytes accessed | tf_op | source)
XLA Modules:
  0.0 75.2 jit_solution(14551135298405378740)
XLA Ops:
  0.6 9.6 %shard_map.85 = (bf16[96,1024]{1,0:T(8,128)(2,1)S(1)}, f32[8,1024]{1,0:T(8,128)S(1)}) custom-call(bf16[512,8192]{1,0:T(8,128)(2,1)} %bitcast.10, bf16[512,8192]{1,0:T(8,128)(2,1)} %bitcast.11, bf16[32,8192]{1,0:T(8,128)(2,1)} %bitcast.12, bf16[32,8192]{1,0:T(8,128)(2,1)} %bitcast.13, s32[1,512]{1,0:T(1,128)} %bitcast.14, s32[1,62]{1,0:T(1,128)} %bitcast.15), custom_call_target="tpu_custom_call" | custom-call | tf_op jit(solution)/shard_map/pallas_call | solution.py:160
  10.2 25.5 %shard_map.86.all_ref = bf16[1024,1024]{1,0:T(8,128)(2,1)S(1)} custom-call(bf16[96,1024]{1,0:T(8,128)(2,1)S(1)} %get-tuple-element.8.arr_ref, f32[8,1024]{1,0:T(8,128)S(1)} %get-tuple-element.9.aux_ref), custom_call_target="tpu_custom_call" | custom-call | tf_op jit(solution)/shard_map/pallas_call | solution.py:308
  35.7 34.0 %shard_map.87 = (f32[1024,1024]{1,0:T(8,128)}, bf16[32,1024]{1,0:T(8,128)(2,1)}, f32[8,128]{1,0:T(8,128)S(1)}) custom-call(bf16[1024,1024]{1,0:T(8,128)(2,1)S(1)} %shard_map.86.all_ref), custom_call_target="tpu_custom_call" | custom-call | tf_op jit(solution)/shard_map/pallas_call | solution.py:413
  69.7 5.0 %shard_map.88 = f32[1,32]{1,0:T(1,128)S(1)} custom-call(f32[8,128]{1,0:T(8,128)S(1)} %get-tuple-element.12.quad_ref), custom_call_target="tpu_custom_call" | custom-call | tf_op jit(solution)/shard_map/pallas_call | solution.py:454
  74.7 0.5 copy.10

commit v4 on v3

--- a/solution.py
+++ b/solution.py
@@ -148,41 +148,9 @@
     aux_ref[...] = aux
 
 
-def front(acts, grads, in_proj, out_proj, segs, moves):
-    tokens, depth = acts.shape
-    kin, kout = in_proj.shape[0], out_proj.shape[0]
-    width = kin * kout
-    slots = -(-(moves.shape[1] + 1) // 16) * 16
-    acts, grads, in_proj, out_proj, segs, moves = (
-        pltpu.with_memory_space_constraint(v, pltpu.HBM) for v in (acts, grads, in_proj, out_proj, segs, moves)
-    )
-    held = pl.BlockSpec(memory_space=pltpu.HBM)
-    return pl.pallas_call(
-        front_kernel,
-        in_specs=[held] * 6,
-        out_specs=(VMEM, VMEM),
-        out_shape=(
-            jax.ShapeDtypeStruct((3 * BAL, width), BF16),
-            jax.ShapeDtypeStruct((8, width), F32),
-        ),
-        scratch_shapes=[
-            pltpu.VMEM(acts.shape, BF16),
-            pltpu.VMEM(grads.shape, BF16),
-            pltpu.VMEM(in_proj.shape, BF16),
-            pltpu.VMEM(out_proj.shape, BF16),
-            pltpu.VMEM(segs.shape, jnp.int32),
-            pltpu.VMEM(moves.shape, jnp.int32),
-            pltpu.VMEM((slots, width), F32),
-            pltpu.VMEM((slots, 128), F32),
-            pltpu.VMEM((1, 128), jnp.int32),
-            pltpu.SemaphoreType.DMA((2, len(CHUNKS))),
-            pltpu.SemaphoreType.DMA((4,)),
-        ],
-        compiler_params=pltpu.CompilerParams(vmem_limit_bytes=40 * 2**20),
-    )(acts, grads, in_proj, out_proj, segs, moves)
-
-
-def gather_kernel(side, cores, arr_ref, aux_ref, all_ref, from_right, from_left, aux_in, ex_send, ex_recv, send, recv):
+def gather_kernel(side, cores, *refs):
+    held, all_ref, work, refs = refs[:6], refs[6], refs[7:18], refs[18:]
+    arr_ref, aux_ref, from_right, from_left, aux_in, ex_send, ex_recv, send, recv = refs
     n_rep = side * side * cores
     width = all_ref.shape[1]
     me = lax.axis_index("rep")
@@ -202,6 +170,7 @@
     senders = [right, left, right2, sibling] + around
     for device in senders:
         pl.semaphore_signal(barrier, inc=1, device_id={"rep": device}, device_id_type=pl.DeviceIdType.MESH)
+    front_kernel(*held, arr_ref, aux_ref, *work)
     pl.semaphore_wait(barrier, len(senders))
 
     def copy(src, dst, s, r, device):
@@ -301,16 +270,35 @@
         c.wait_send()
 
 
-def gather(arr, aux, n_rep):
-    width = arr.shape[1]
+def gather(acts, grads, in_proj, out_proj, segs, moves, n_rep):
+    kin, kout = in_proj.shape[0], out_proj.shape[0]
+    width = kin * kout
+    slots = -(-(moves.shape[1] + 1) // 16) * 16
     cores = 2
     side = round((n_rep // cores) ** 0.5)
+    held = [
+        pltpu.with_memory_space_constraint(v, pltpu.HBM)
+        for v in (acts, grads, in_proj, out_proj, segs, moves)
+    ]
     return pl.pallas_call(
         functools.partial(gather_kernel, side, cores),
         out_shape=jax.ShapeDtypeStruct((BAL * n_rep, width), BF16),
-        in_specs=[VMEM, VMEM],
+        in_specs=[pl.BlockSpec(memory_space=pltpu.HBM)] * 6,
         out_specs=VMEM,
         scratch_shapes=[
+            pltpu.VMEM(acts.shape, BF16),
+            pltpu.VMEM(grads.shape, BF16),
+            pltpu.VMEM(in_proj.shape, BF16),
+            pltpu.VMEM(out_proj.shape, BF16),
+            pltpu.VMEM(segs.shape, jnp.int32),
+            pltpu.VMEM(moves.shape, jnp.int32),
+            pltpu.VMEM((slots, width), F32),
+            pltpu.VMEM((slots, 128), F32),
+            pltpu.VMEM((1, 128), jnp.int32),
+            pltpu.SemaphoreType.DMA((2, len(CHUNKS))),
+            pltpu.SemaphoreType.DMA((4,)),
+            pltpu.VMEM((3 * BAL, width), BF16),
+            pltpu.VMEM((8, width), F32),
             pltpu.VMEM((BAL, width), BF16),
             pltpu.VMEM((BAL, width), BF16),
             pltpu.VMEM((3, 8, width), F32),
@@ -320,37 +308,61 @@
             pltpu.SemaphoreType.DMA((62,)),
         ],
         compiler_params=pltpu.CompilerParams(
-            collective_id=0, has_side_effects=True, vmem_limit_bytes=16 * 2**20
+            collective_id=0, has_side_effects=True, vmem_limit_bytes=40 * 2**20
         ),
-    )(arr, aux)
-
-
-def pivot_rows(D, V):
+    )(*held)
+
+SUB = 16
+
+def pivot_rows(V, at):
     size, width = V.shape
     tiles, strips = size // 8, width // 128
     row = iota((8, 128), 0)
-    cols = [
-        [jnp.broadcast_to(D[8 * i : 8 * i + 8, j : j + 1], (8, 128)) if i >= j // 8 else None for i in range(tiles)]
-        for j in range(size)
-    ]
     rows = [[V[8 * i : 8 * i + 8, 128 * c : 128 * c + 128] for c in range(strips)] for i in range(tiles)]
     pivots = [jnp.ones((8, 128), F32) for _ in range(tiles)]
-    for j in range(size):
+    cols = {}
+
+    def element(column, j):
+        return jnp.broadcast_to(column[j // 8][j % 8 : j % 8 + 1], (8, 128))
+
+    for j in range(0, size, 2):
         tile, sub = divmod(j, 8)
-        column = cols[j]
-        pivot = jnp.broadcast_to(column[tile][sub : sub + 1], (8, 128))
-        inverse = 1.0 / pivot
-        pivots[tile] = jnp.where(row == sub, pivot, pivots[tile])
-        factor = [column[i] * inverse if i >= tile else None for i in range(tiles)]
-        for j2 in range(j + 1, size):
-            other = jnp.broadcast_to(column[j2 // 8][j2 % 8 : j2 % 8 + 1], (8, 128))
+        if j % SUB == 0:
+            for k in range(j, j + SUB):
+                lanes = slice(at + k, at + k + 1)
+                cols[k] = [
+                    jnp.broadcast_to(rows[i][0][:, lanes], (8, 128)) if i >= k // 8 else None for i in range(tiles)
+                ]
+        one, two = cols[j], cols[j + 1]
+        p, q, r = element(one, j), element(one, j + 1), element(two, j + 1)
+        det = p * r - q * q
+        inv_p = 1.0 / p
+        inv_det = 1.0 / det
+        ratio = q * inv_p
+        second = p * inv_det
+        pivots[tile] = jnp.where(row == sub, p, pivots[tile])
+        pivots[tile] = jnp.where(row == sub + 1, det * inv_p, pivots[tile])
+        left = [None] * tiles
+        right = [None] * tiles
+        rest = [None] * tiles
+        for i in range(tile, tiles):
+            rest[i] = two[i] - one[i] * ratio
+            left[i] = one[i] * inv_p
+            right[i] = rest[i] * second
+        for j2 in range(j + 2, j - j % SUB + SUB):
+            mul_one, mul_two = element(one, j2), element(rest, j2)
             for i in range(j2 // 8, tiles):
-                cols[j2][i] = cols[j2][i] - factor[i] * other
+                cols[j2][i] = (cols[j2][i] - left[i] * mul_one) - right[i] * mul_two
         for c in range(strips):
-            source = jnp.broadcast_to(rows[tile][c][sub : sub + 1], (8, 128))
+            top = jnp.broadcast_to(rows[tile][c][sub : sub + 1], (8, 128))
+            next_row = jnp.broadcast_to(rows[tile][c][sub + 1 : sub + 2], (8, 128)) - top * ratio
             for i in range(tile, tiles):
-                weight = jnp.where(row > sub, factor[i], 0.0) if i == tile else factor[i]
-                rows[i][c] = rows[i][c] - weight * source
+                if i == tile:
+                    wl = jnp.where(row > sub, left[i], 0.0)
+                    wr = jnp.where(row > sub + 1, right[i], 0.0)
+                else:
+                    wl, wr = left[i], right[i]
+                rows[i][c] = (rows[i][c] - wl * top) - wr * next_row
     out = []
     for i in range(tiles):
         scale = lax.rsqrt(pivots[i])
@@ -363,7 +375,7 @@
     V = jnp.concatenate([A, onehot(same, F32)], axis=1)
     done = []
     for at in range(0, BLOCK, GROUP):
-        rows = pivot_rows(V[:GROUP, at : at + GROUP], V[:GROUP])
+        rows = pivot_rows(V[:GROUP], at)
         done.append(rows)
         if at + GROUP < BLOCK:
             hi, lo = split(rows)
@@ -468,11 +480,10 @@
 
 
 def on_device(n_rep, layers, activations, output_grads, in_projection, out_projection, segment_ids, move_list):
-    arranged, aux = front(
+    everyone = gather(
         activations[0], output_grads[0], in_projection[0], out_projection[0],
-        segment_ids[None], move_list[None],
+        segment_ids[None], move_list[None], n_rep,
     )
-    everyone = gather(arranged, aux, n_rep)
     upper, mine, quad = factor(everyone)
     influence = layer_sum(quad, layers)
     return (upper[None], mine[None], influence[0])

time: 75.3 us -> 67.5 us (0.90)
  Pallas kernels: 74.1 us -> 66.2 us
    pallas_call x1 -> x0, Pallas kernels: 9.6 us -> none  [front(): pl.pallas_call(front_kernel, in_specs=[held] * 6, out_specs=(VMEM, VMEM),...]
    pallas_call x1, Pallas kernels: 25.5 us -> 31.3 us  [gather(): pl.pallas_call(functools.partial(gather_kernel, side, cores), out_shape=j...]
    pallas_call x1, Pallas kernels: 34 us -> 30.1 us  [factor(): pl.pallas_call(factor_kernel, out_shape=(jax.ShapeDtypeStruct((n, n), F32...]
where the time goes in v4:
time: 67.5 us; the launch traced here: 67.4 us
  Pallas kernels  66.2 us (98%)
    pallas_call x1, Pallas kernels, gather(): pl.pallas_call(functools.partial(gather_kernel, side, cores), out_shape=j...  31.3 us
    pallas_call x1, Pallas kernels, factor(): pl.pallas_call(factor_kernel, out_shape=(jax.ShapeDtypeStruct((n, n), F32...  30.1 us
    pallas_call x1, Pallas kernels, layer_sum(): pl.pallas_call(functools.partial(layer_sum_kernel, layers), out_shape=jax...  4.82 us

profile of v4, /device:TPU:1, one launch (start us, length us, event | category | flops | bytes accessed | tf_op | source)
XLA Modules:
  0.0 67.4 jit_solution(16417165309656885211)
XLA Ops:
  0.6 31.3 %shard_map.85.all_ref = bf16[1024,1024]{1,0:T(8,128)(2,1)S(1)} custom-call(bf16[512,8192]{1,0:T(8,128)(2,1)} %bitcast.10, bf16[512,8192]{1,0:T(8,128)(2,1)} %bitcast.11, bf16[32,8192]{1,0:T(8,128)(2,1)} %bitcast.12, bf16[32,8192]{1,0:T(8,128)(2,1)} %bitcast.13, s32[1,512]{1,0:T(1,128)} %bitcast.14, s32[1,62]{1,0:T(1,128)} %bitcast.15), custom_call_target="tpu_custom_call" | custom-call | tf_op jit(solution)/shard_map/pallas_call | solution.py:283
  32.0 30.1 %shard_map.86 = (f32[1024,1024]{1,0:T(8,128)}, bf16[32,1024]{1,0:T(8,128)(2,1)}, f32[8,128]{1,0:T(8,128)S(1)}) custom-call(bf16[1024,1024]{1,0:T(8,128)(2,1)S(1)} %shard_map.85.all_ref), custom_call_target="tpu_custom_call" | custom-call | tf_op jit(solution)/shard_map/pallas_call | solution.py:425
  62.0 4.8 %shard_map.87 = f32[1,32]{1,0:T(1,128)S(1)} custom-call(f32[8,128]{1,0:T(8,128)S(1)} %get-tuple-element.8.quad_ref), custom_call_target="tpu_custom_call" | custom-call | tf_op jit(solution)/shard_map/pallas_call | solution.py:466
  66.8 0.5 copy.10

commit v5 on v4

--- a/solution.py
+++ b/solution.py
@@ -312,7 +312,8 @@
         ),
     )(*held)
 
-SUB = 16
+AHEAD_COLS = 6
+SUB = 8
 
 def pivot_rows(V, at):
     size, width = V.shape
@@ -325,14 +326,20 @@
     def element(column, j):
         return jnp.broadcast_to(column[j // 8][j % 8 : j % 8 + 1], (8, 128))
 
+    def spread(first, stop):
+        for k in range(first, stop):
+            lanes = slice(at + k, at + k + 1)
+            cols[k] = [
+                jnp.broadcast_to(rows[i][0][:, lanes], (8, 128)) if i >= k // 8 else None for i in range(tiles)
+            ]
+
     for j in range(0, size, 2):
         tile, sub = divmod(j, 8)
-        if j % SUB == 0:
-            for k in range(j, j + SUB):
-                lanes = slice(at + k, at + k + 1)
-                cols[k] = [
-                    jnp.broadcast_to(rows[i][0][:, lanes], (8, 128)) if i >= k // 8 else None for i in range(tiles)
-                ]
+        end = j - j % SUB + SUB
+        if j == 0:
+            spread(0, SUB)
+        if j == end - AHEAD_COLS and end < size:
+            spread(end, end + SUB)
         one, two = cols[j], cols[j + 1]
         p, q, r = element(one, j), element(one, j + 1), element(two, j + 1)
         det = p * r - q * q
@@ -349,7 +356,7 @@
             rest[i] = two[i] - one[i] * ratio
             left[i] = one[i] * inv_p
             right[i] = rest[i] * second
-        for j2 in range(j + 2, j - j % SUB + SUB):
+        for j2 in [k for k in sorted(cols) if k > j + 1]:
             mul_one, mul_two = element(one, j2), element(rest, j2)
             for i in range(j2 // 8, tiles):
                 cols[j2][i] = (cols[j2][i] - left[i] * mul_one) - right[i] * mul_two
@@ -379,35 +386,64 @@
         done.append(rows)
         if at + GROUP < BLOCK:
             hi, lo = split(rows)
-            here = jnp.concatenate([hi, hi, lo], axis=0)[:, at + GROUP : BLOCK]
-            V = V[GROUP:] - dot_t(here, jnp.concatenate([hi, lo, hi], axis=0))
+            here = jnp.concatenate([hi, hi, lo], axis=0)
+            update = dot_t(here[:, :BLOCK], jnp.concatenate([hi, lo, hi], axis=0))
+            V = V[GROUP:] - update[at + GROUP :]
     both = jnp.concatenate(done, axis=0)
     return both[:, :BLOCK], both[:, BLOCK:]
 
 
-def factor_kernel(all_ref, fac_ref, mine_ref, quad_ref, high, low):
+def product(lh, ll, gh, gl):
+    left = jnp.concatenate([lh, lh, ll], axis=0)
+    return dot_t(left, jnp.concatenate([gh, gl, gh], axis=0))
+
+
+def solve(inverse, columns):
+    th, tl = split(inverse)
+    sh, sl = split(columns)
+    return dot(jnp.concatenate([th, th, tl], axis=1), jnp.concatenate([sh, sl, sh], axis=0))
+
+
+def factor_kernel(all_ref, fac_hbm, mine_hbm, quad_ref, fac_ref, high, low, sem):
     docs, n = all_ref.shape
     width = n + 128
     replica = lax.axis_index("rep")
-    mine = all_ref[pl.ds(pl.multiple_of(replica * BAL, BAL), BAL), :]
-    mine_ref[...] = mine
+    own = pl.ds(pl.multiple_of(replica * BAL, BAL), BAL)
+    mine = all_ref[own, :]
+    writes = [pltpu.make_async_copy(all_ref.at[own], mine_hbm, sem.at[n // BLOCK])]
+    writes[0].start()
     ri, ci = iota((BLOCK, BLOCK), 0), iota((BLOCK, BLOCK), 1)
     quad = jnp.zeros((1, 128), F32)
-    for a in range(0, n, BLOCK):
-        b = a + BLOCK
+
+    def open_panel(a):
+        b, before = a + BLOCK, a - BLOCK
         hessian = dot_t(all_ref[:, a:b], all_ref[:, a:n]) * (1.0 / docs)
         extra = mine[:, a:b].astype(F32).T
         extra = jnp.concatenate([extra, jnp.zeros((BLOCK, 128 - BAL), F32)], axis=1)
         panel = jnp.concatenate([hessian, extra], axis=1)
+        if before > 0:
+            lh, ll = high[:before, a:b], low[:before, a:b]
+            gh, gl = high[:before, a:width], low[:before, a:width]
+            panel = panel - (dot_t(lh, gh) + dot_t(lh, gl) + dot_t(ll, gh))
+        return panel
+
+    following = open_panel(0)
+    for a in range(0, n, BLOCK):
+        b = a + BLOCK
+        diag, rest = following[:, :BLOCK], following[:, BLOCK:]
         if a > 0:
-            lh, ll = high[:a, a:b], low[:a, a:b]
-            gh, gl = high[:a, a:width], low[:a, a:width]
-            panel = panel - (dot_t(lh, gh) + dot_t(lh, gl) + dot_t(ll, gh))
-        upper, inverse = factor_block(panel[:, :BLOCK] + jnp.where(ri == ci, DAMPING, 0.0))
+            lh, ll = hi[:, :BLOCK], lo[:, :BLOCK]
+            diag = diag - product(lh, ll, lh, ll)
+        if b < n:
+            following = open_panel(b)
+        upper, inverse = factor_block(diag + jnp.where(ri == ci, DAMPING, 0.0))
+        if a > 0:
+            rest = rest - product(lh, ll, hi[:, BLOCK:], lo[:, BLOCK:])
         fac_ref[a:b, a:b] = jnp.where(ci >= ri, upper, 0.0)
-        th, tl = split(inverse)
-        sh, sl = split(panel[:, BLOCK:])
-        solved = dot(th, sh) + dot(th, sl) + dot(tl, sh)
+        parts = [solve(inverse, rest[:, :BLOCK])]
+        if b < n:
+            parts.append(solve(inverse, rest[:, BLOCK:]))
+        solved = jnp.concatenate(parts, axis=1)
         if b < n:
             fac_ref[a:b, b:n] = solved[:, : n - b]
             hi, lo = split(solved)
@@ -415,9 +451,14 @@
             low[a:b, b:width] = lo
         if a > 0:
             fac_ref[a:b, :a] = jnp.zeros((BLOCK, a), F32)
+        done = pl.ds(a, BLOCK)
+        writes.append(pltpu.make_async_copy(fac_ref.at[done], fac_hbm.at[done], sem.at[a // BLOCK]))
+        writes[-1].start()
         tail = solved[:, n - b :]
         quad = quad + jnp.sum(tail * tail, axis=0, keepdims=True)
     quad_ref[...] = jnp.broadcast_to(quad * (1.0 / n), quad_ref.shape)
+    for write in writes:
+        write.wait()
 
 
 def factor(everyone):
@@ -430,8 +471,13 @@
             jax.ShapeDtypeStruct((8, 128), F32),
         ),
         in_specs=[VMEM],
-        out_specs=(VMEM, VMEM, VMEM),
-        scratch_shapes=[pltpu.VMEM((n, n + 128), BF16), pltpu.VMEM((n, n + 128), BF16)],
+        out_specs=(pl.BlockSpec(memory_space=pltpu.HBM), pl.BlockSpec(memory_space=pltpu.HBM), VMEM),
+        scratch_shapes=[
+            pltpu.VMEM((n, n), F32),
+            pltpu.VMEM((n, n + 128), BF16),
+            pltpu.VMEM((n, n + 128), BF16),
+            pltpu.SemaphoreType.DMA((n // BLOCK + 1,)),
+        ],
         compiler_params=pltpu.CompilerParams(vmem_limit_bytes=40 * 2**20),
     )(everyone)
 

time: 67.5 us -> 62 us (0.919)
  Pallas kernels: 66.2 us -> 60.7 us
    pallas_call x1, Pallas kernels: 30.1 us -> 24.5 us  [factor(): pl.pallas_call(factor_kernel, out_shape=(jax.ShapeDtypeStruct((n, n), F32...]
where the time goes in v5:
time: 62 us; the launch traced here: 61.9 us
  Pallas kernels  60.7 us (98%)
  between operations  0.66 us (1%)
    pallas_call x1, Pallas kernels, gather(): pl.pallas_call(functools.partial(gather_kernel, side, cores), out_shape=j...  31.3 us
    pallas_call x1, Pallas kernels, factor(): pl.pallas_call(factor_kernel, out_shape=(jax.ShapeDtypeStruct((n, n), F32...  24.5 us
    pallas_call x1, Pallas kernels, layer_sum(): pl.pallas_call(functools.partial(layer_sum_kernel, layers), out_shape=jax...  4.92 us

profile of v5, /device:TPU:1, one launch (start us, length us, event | category | flops | bytes accessed | tf_op | source)
XLA Modules:
  0.0 61.9 jit_solution(2902711847442595702)
XLA Ops:
  0.6 31.3 %shard_map.85.all_ref = bf16[1024,1024]{1,0:T(8,128)(2,1)S(1)} custom-call(bf16[512,8192]{1,0:T(8,128)(2,1)} %bitcast.10, bf16[512,8192]{1,0:T(8,128)(2,1)} %bitcast.11, bf16[32,8192]{1,0:T(8,128)(2,1)} %bitcast.12, bf16[32,8192]{1,0:T(8,128)(2,1)} %bitcast.13, s32[1,512]{1,0:T(1,128)} %bitcast.14, s32[1,62]{1,0:T(1,128)} %bitcast.15), custom_call_target="tpu_custom_call" | custom-call | tf_op jit(solution)/shard_map/pallas_call | solution.py:283
  32.0 24.5 %shard_map.86 = (f32[1024,1024]{1,0:T(8,128)}, bf16[32,1024]{1,0:T(8,128)(2,1)}, f32[8,128]{1,0:T(8,128)S(1)}) custom-call(bf16[1024,1024]{1,0:T(8,128)(2,1)S(1)} %shard_map.85.all_ref), custom_call_target="tpu_custom_call" | custom-call | tf_op jit(solution)/shard_map/pallas_call | solution.py:466
  56.4 4.9 %shard_map.87 = f32[1,32]{1,0:T(1,128)S(1)} custom-call(f32[8,128]{1,0:T(8,128)S(1)} %get-tuple-element.8.quad_ref), custom_call_target="tpu_custom_call" | custom-call | tf_op jit(solution)/shard_map/pallas_call | solution.py:512
  61.4 0.5 copy.10

commit v6 on v5

--- a/solution.py
+++ b/solution.py
@@ -94,7 +94,8 @@
         slot = jnp.where(slot == doc_slots, -1, slot)
         member = onehot(slot == here, F32)
         member_low = member.astype(BF16)
-        part = dot(member_low, hi) + dot(member_low, lo)
+        twice = jnp.concatenate([member_low, member_low], axis=1)
+        part = dot(twice, jnp.concatenate([hi, lo], axis=0))
         number = jnp.broadcast_to(jnp.sum(member, axis=1, keepdims=True), counts.shape)
         if c == 0:
             sums[...] = part
@@ -138,14 +139,14 @@
     is_last = iota(counts.shape, 0) == last
     last_count = jnp.sum(jnp.where(is_last, count, 0.0), axis=0, keepdims=True)
     goes_to = jnp.sum(jnp.where(iota(moves.shape, 1) == last, moves, 0), axis=1, keepdims=True)
-    row = iota((8, width), 0)
-    wide = [last_sum, total[doc_slots : doc_slots + 1]]
-    wide += [jnp.broadcast_to(v[:, :1], (1, width)) for v in (last_count, count[doc_slots : doc_slots + 1])]
-    wide += [jnp.broadcast_to(goes_to.astype(F32), (1, width))]
-    aux = jnp.zeros((8, width), F32)
-    for i, v in enumerate(wide):
-        aux = jnp.where(row == i, v, aux)
-    aux_ref[...] = aux
+    tail = iota((8, 128), 0)
+    facts = jnp.where(tail == 0, last_count, jnp.where(tail == 1, count[doc_slots : doc_slots + 1], goes_to.astype(F32)))
+    folded = [
+        v[:, 128 * i : 128 * i + 128]
+        for v in (last_sum, total[doc_slots : doc_slots + 1])
+        for i in range(width // 128)
+    ]
+    aux_ref[...] = jnp.concatenate(folded + [facts], axis=0)
 
 
 def gather_kernel(side, cores, *refs):
@@ -196,10 +197,13 @@
     after, before, after2 = aux_in[0], aux_in[1], aux_in[2]
     row = iota((BAL, width), 0).astype(F32)
     base = (me * BAL).astype(F32)
+    folds = width // 128
     for a, b in ((before, own), (own, after), (after, after2)):
-        length = jnp.maximum(a[2:3] + b[3:4], 1.0)
-        feature = (a[0:1] + b[1:2]) * (1.0 / jnp.sqrt(length))
-        mine = jnp.where(row == a[4:5] - base, feature, mine)
+        facts_a, facts_b = a[2 * folds :], b[2 * folds :]
+        length = jnp.maximum(facts_a[0:1] + facts_b[1:2], 1.0)
+        feature = (a[:folds] + b[folds : 2 * folds]) * (1.0 / jnp.sqrt(length))
+        feature = jnp.concatenate([feature[i : i + 1] for i in range(folds)], axis=1)
+        mine = jnp.where(row == facts_a[2:3, :1] - base, feature, mine)
     all_ref[pl.ds(pl.multiple_of(me * BAL, BAL), BAL), :] = mine.astype(BF16)
 
     half = width // 2
@@ -298,10 +302,10 @@
             pltpu.SemaphoreType.DMA((2, len(CHUNKS))),
             pltpu.SemaphoreType.DMA((4,)),
             pltpu.VMEM((3 * BAL, width), BF16),
-            pltpu.VMEM((8, width), F32),
+            pltpu.VMEM((width // 64 + 8, 128), F32),
             pltpu.VMEM((BAL, width), BF16),
             pltpu.VMEM((BAL, width), BF16),
-            pltpu.VMEM((3, 8, width), F32),
+            pltpu.VMEM((3, width // 64 + 8, 128), F32),
             pltpu.SemaphoreType.DMA((5,)),
             pltpu.SemaphoreType.DMA((5,)),
             pltpu.SemaphoreType.DMA((62,)),
@@ -417,7 +421,11 @@
 
     def open_panel(a):
         b, before = a + BLOCK, a - BLOCK
-        hessian = dot_t(all_ref[:, a:b], all_ref[:, a:n]) * (1.0 / docs)
+        left = all_ref[:, a:b]
+        hessian = dot_t(left, left)
+        if b < n:
+            hessian = jnp.concatenate([hessian, dot_t(left, all_ref[:, b:n])], axis=1)
+        hessian = hessian * (1.0 / docs)
         extra = mine[:, a:b].astype(F32).T
         extra = jnp.concatenate([extra, jnp.zeros((BLOCK, 128 - BAL), F32)], axis=1)
         panel = jnp.concatenate([hessian, extra], axis=1)

time: 62 us -> 61.5 us (level)
  no operation moved by 1% of the time
where the time goes in v6:
time: 61.5 us; the launch traced here: 61.4 us
  Pallas kernels  60.2 us (98%)
  between operations  0.66 us (1%)
    pallas_call x1, Pallas kernels, gather(): pl.pallas_call(functools.partial(gather_kernel, side, cores), out_shape=j...  31 us
    pallas_call x1, Pallas kernels, factor(): pl.pallas_call(factor_kernel, out_shape=(jax.ShapeDtypeStruct((n, n), F32...  24.3 us
    pallas_call x1, Pallas kernels, layer_sum(): pl.pallas_call(functools.partial(layer_sum_kernel, layers), out_shape=jax...  4.91 us

profile of v6, /device:TPU:1, one launch (start us, length us, event | category | flops | bytes accessed | tf_op | source)
XLA Modules:
  0.0 61.4 jit_solution(1769617857848729567)
XLA Ops:
  0.6 31.0 %shard_map.85.all_ref = bf16[1024,1024]{1,0:T(8,128)(2,1)S(1)} custom-call(bf16[512,8192]{1,0:T(8,128)(2,1)} %bitcast.10, bf16[512,8192]{1,0:T(8,128)(2,1)} %bitcast.11, bf16[32,8192]{1,0:T(8,128)(2,1)} %bitcast.12, bf16[32,8192]{1,0:T(8,128)(2,1)} %bitcast.13, s32[1,512]{1,0:T(1,128)} %bitcast.14, s32[1,62]{1,0:T(1,128)} %bitcast.15), custom_call_target="tpu_custom_call" | custom-call | tf_op jit(solution)/shard_map/pallas_call | solution.py:287
  31.7 24.3 %shard_map.86 = (f32[1024,1024]{1,0:T(8,128)}, bf16[32,1024]{1,0:T(8,128)(2,1)}, f32[8,128]{1,0:T(8,128)S(1)}) custom-call(bf16[1024,1024]{1,0:T(8,128)(2,1)S(1)} %shard_map.85.all_ref), custom_call_target="tpu_custom_call" | custom-call | tf_op jit(solution)/shard_map/pallas_call | solution.py:474
  56.0 4.9 %shard_map.87 = f32[1,32]{1,0:T(1,128)S(1)} custom-call(f32[8,128]{1,0:T(8,128)S(1)} %get-tuple-element.8.quad_ref), custom_call_target="tpu_custom_call" | custom-call | tf_op jit(solution)/shard_map/pallas_call | solution.py:520
  60.9 0.5 copy.10
